TPU v7x, 1024 devices: a whole 4x8x16 slice. The times are simulated.
1024 devices in a mesh: seq: 64 (over z, x), head: 16 (over y, core).
Axes of the slice: x: 4, y: 8, z: 16, core: 2. Of those that a mesh axis runs over, the one named last changes fastest.
Arguments:
- query_rows: bfloat16 [65536, 16, 128], P('seq', 'head'), may hold values from -130 to 130
- key_rows: bfloat16 [65536, 16, 128], P('seq', 'head'), may hold values from -0.52734375 to 0.52734375
- value_rows: bfloat16 [65536, 16, 128], P('seq', 'head'), may hold values from -6 to 6
- log_gate: float32 [16, 65536], P('head', 'seq'), may hold values from -1 to 0
- norm_gain: float32 [16, 128], P('head'), may hold values from 0.5 to 1.5
- doc_ends: int32 [4096], P('seq'), may hold values from 0 to 1024, as said below
- doc_page: int32 [4096], replicated, may hold values from -1 to 4095, as said below
Outputs:
- attended: bfloat16 [65536, 16, 128], P('seq', 'head')
- state_cache: bfloat16 [4096, 16, 128, 128], P('seq', 'head')
Inputs may be any that keep to these rules, and one draw needn't show every extreme that they name: `doc_ends`: index s of seq holds entries s * 64 to s * 64 + 63: its nonzero entries come first and rise strictly. An entry e means that a document ends after local token e - 1 and, if e < 1024, a new one starts at local token e; zeros are unused. Some index of seq uses all 64 entries and some index uses none. `doc_page`: entry i is the cache page, owned by index page // 64 of seq, that receives the state of the document ended by doc_ends entry i, and -1 exactly where that entry is 0. No page is named twice, and the documents ending on one index of seq go to different owners.
All inputs are finite; a program needn't handle non-finite values.
Results may differ from a plain program's by a relative error of at most 0.0044.
Values may be sent and summed in bfloat16 or wider, within the bound.
A program may use at most 32 MiB of HBM per device.

v0:
```python
import math

import jax
import jax.numpy as jnp
from jax import lax
from jax.sharding import PartitionSpec as P

SPAN = 512


epsilon = 1e-05
precise = lax.Precision.HIGHEST


def carried_in(value, axis, join, neutral):
    count, mine = (lax.axis_size(axis), lax.axis_index(axis))
    pieces = jax.tree.map(lambda part: lax.all_gather(part, axis), value)
    total = jax.tree.map(
        lambda part, zero: jnp.full_like(part, 0) + jnp.asarray(zero, part.dtype), value, neutral
    )

    def turn(position, total):
        longer = join(total, jax.tree.map(lambda part: part[position], pieces))
        return jax.tree.map(lambda new, old: jnp.where(position < mine, new, old), longer, total)

    return lax.fori_loop(0, count - 1, turn, total)


def block_weights(query_block, key_block, running_total, segment_block):
    length = segment_block.shape[0]
    slot_positions = jnp.arange(length, dtype=jnp.int32)
    allowed = (slot_positions[:, None] >= slot_positions[None, :]) & (
        segment_block[:, None] == segment_block[None, :]
    )
    spread = running_total[:, :, None] - running_total[:, None, :]
    damping = jnp.exp(jnp.where(allowed[None], spread, -jnp.inf))
    scores = jnp.einsum("thd,shd->hts", query_block, key_block, preferred_element_type=jnp.float32)
    return (scores * damping).astype(jnp.bfloat16)


def row_weights(running_total, segment_block, seg_before, row_index):
    length = segment_block.shape[0]
    slot_positions = jnp.arange(length, dtype=jnp.int32)
    segment_row = segment_block[row_index]
    row_level = running_total[:, row_index]
    allowed = (slot_positions <= row_index) & (segment_block == segment_row)
    weights = jnp.exp(jnp.where(allowed[None, :], row_level[:, None] - running_total, -jnp.inf))
    carry_keep = jnp.where(segment_row == seg_before, jnp.exp(row_level), 0.0)
    return (weights, carry_keep)


def row_state(
    entry_state, key_block, value_block, running_total, segment_block, seg_before, row_index
):
    weights, carry_keep = row_weights(running_total, segment_block, seg_before, row_index)
    scaled = key_block.astype(jnp.float32) * weights.T[:, :, None]
    fresh = jnp.einsum("shd,shv->hdv", scaled, value_block.astype(jnp.float32), precision=precise)
    return carry_keep[:, None, None] * entry_state + fresh


def end_state(
    entry_state, key_block, value_block, running_total, segment_block, seg_before, row_index
):
    weights, carry_keep = row_weights(running_total, segment_block, seg_before, row_index)
    decayed = (key_block.astype(jnp.float32) * weights.T[:, :, None]).astype(jnp.bfloat16)
    fresh = jnp.einsum("shd,shv->hdv", decayed, value_block, preferred_element_type=jnp.float32)
    return carry_keep[:, None, None] * entry_state + fresh


def block_step(carry_in, inputs):
    state_in, seg_before = carry_in
    query_block, key_block, value_block, gate_block, segment_block = inputs
    running_total = jnp.cumsum(gate_block, axis=1)
    weights = block_weights(query_block, key_block, running_total, segment_block)
    within_block = jnp.einsum(
        "hts,shv->thv", weights, value_block, preferred_element_type=jnp.float32
    )
    carry_reach = jnp.where((segment_block == seg_before)[None, :], jnp.exp(running_total), 0.0)
    from_before = (
        jnp.einsum("thd,hdv->thv", query_block.astype(jnp.float32), state_in, precision=precise)
        * carry_reach.T[:, :, None]
    )
    new_state = row_state(
        state_in,
        key_block,
        value_block,
        running_total,
        segment_block,
        seg_before,
        segment_block.shape[0] - 1,
    )
    return ((new_state, segment_block[-1]), (within_block + from_before, state_in))


def shards(query_rows, key_rows, value_rows, log_gate, norm_gain, doc_ends, doc_page):
    tokens, heads, depth = query_rows.shape
    width = value_rows.shape[2]
    blocks = tokens // SPAN
    bounds = doc_ends.shape[0]
    devices = lax.axis_size("seq")
    rank_here = lax.axis_index("seq")
    positions = jnp.arange(tokens, dtype=jnp.int32)
    inside = (doc_ends > 0) & (doc_ends < tokens)
    segment = jnp.sum(
        (inside[:, None] & (doc_ends[:, None] <= positions[None, :])).astype(jnp.int32), axis=0
    )
    inputs = (
        query_rows.reshape(blocks, SPAN, heads, depth),
        key_rows.reshape(blocks, SPAN, heads, depth),
        value_rows.reshape(blocks, SPAN, heads, width),
        log_gate.reshape(heads, blocks, SPAN).transpose(1, 0, 2),
        segment.reshape(blocks, SPAN),
    )
    initial = (jnp.zeros((heads, depth, width), jnp.float32), jnp.zeros((), jnp.int32))
    (final_state, last_segment), (local_out, entries) = lax.scan(block_step, initial, inputs)
    local_out = local_out.reshape(tokens, heads, width)
    running = jnp.cumsum(log_gate, axis=1)
    any_ended = jnp.any(doc_ends > 0)
    at_edge = jnp.any(doc_ends == tokens)
    through = jnp.where(any_ended, 0.0, jnp.exp(running[:, -1]))
    state_out = jnp.where(at_edge, 0.0, final_state)

    def combine(earlier_part, later_part):
        return (
            earlier_part[0] * later_part[0],
            later_part[0][:, None, None] * earlier_part[1] + later_part[1],
        )

    identity = (jnp.ones_like(through), jnp.zeros_like(state_out))
    carry_state = carried_in((through, state_out), "seq", combine, identity)[1]
    carry_reach = jnp.where((segment == 0)[None, :], jnp.exp(running), 0.0)
    carried_out = jnp.einsum(
        "thd,hdv->thv", query_rows.astype(jnp.float32), carry_state, precision=precise
    )
    mixed_out = local_out + carried_out * carry_reach.T[:, :, None]
    squares = lax.psum(jnp.sum(mixed_out * mixed_out, axis=(1, 2)), "head")
    norm_scale = lax.rsqrt(squares / (heads * lax.axis_size("head") * width) + epsilon)
    attended = (mixed_out * norm_scale[:, None, None] * norm_gain[None]).astype(jnp.bfloat16)

    def finished_state(ending):
        row_local = jnp.maximum(ending, 1) - 1
        block_index = row_local // SPAN
        first_row = block_index * SPAN
        key_block = lax.dynamic_slice_in_dim(key_rows, first_row, SPAN, 0)
        value_block = lax.dynamic_slice_in_dim(value_rows, first_row, SPAN, 0)
        gate_block = lax.dynamic_slice_in_dim(log_gate, first_row, SPAN, 1)
        segment_block = lax.dynamic_slice_in_dim(segment, first_row, SPAN, 0)
        seg_before = jnp.where(block_index > 0, segment[jnp.maximum(first_row - 1, 0)], 0)
        local_state = end_state(
            entries[block_index],
            key_block,
            value_block,
            jnp.cumsum(gate_block, axis=1),
            segment_block,
            seg_before,
            row_local - first_row,
        )
        carry_link = jnp.where(segment[row_local] == 0, jnp.exp(running[:, row_local]), 0.0)
        return (local_state + carry_link[:, None, None] * carry_state).astype(jnp.bfloat16)

    end_group = math.gcd(bounds, 8)
    grouped_ends = doc_ends.reshape(bounds // end_group, end_group)
    finished = lax.map(jax.vmap(finished_state), grouped_ends).reshape(bounds, heads, depth, width)
    own_pages = lax.dynamic_slice_in_dim(doc_page, rank_here * bounds, bounds, 0)
    owners = jnp.where(own_pages >= 0, own_pages // devices, -1)
    receivers = jnp.arange(devices, dtype=jnp.int32)
    routing = (owners[None, :] == receivers[:, None]).astype(jnp.bfloat16)
    outgoing = jnp.einsum(
        "ob,bhkv->ohkv", routing, finished, preferred_element_type=jnp.float32
    ).astype(jnp.bfloat16)
    incoming = lax.all_to_all(outgoing, "seq", split_axis=0, concat_axis=0, tiled=True)
    page_table = doc_page.reshape(devices, bounds)
    page_ids = rank_here * devices + jnp.arange(devices, dtype=jnp.int32)
    placing = jnp.any(page_table[None, :, :] == page_ids[:, None, None], axis=2).astype(
        jnp.bfloat16
    )
    state_cache = jnp.einsum(
        "ps,shkv->phkv", placing, incoming, preferred_element_type=jnp.float32
    ).astype(jnp.bfloat16)
    return (attended, state_cache)


def solution(mesh):
    placed = (
        P("seq", "head", None),
        P("seq", "head", None),
        P("seq", "head", None),
        P("head", "seq"),
        P("head", None),
        P("seq"),
        P(),
    )
    return jax.shard_map(
        shards,
        mesh=mesh,
        in_specs=placed,
        out_specs=(P("seq", "head", None), P("seq", "head", None, None)),
        check_vma=False,
    )
```

profile of v0, /device:TPU:56, one launch (start us, length us, event | category | flops | bytes accessed | tf_op | source)
XLA Modules:
  0.0 859.5 jit_solution(5975546880464911134)
XLA Ops:
  9.4 22.8 %while.59 = (s32[]{:T(128)}, f32[1,128,128]{2,1,0:T(8,128)S(1)}, s32[]{:T(128)}, f32[2,512,1,128]{1,0,3,2:T(2,128)S(1)}, f32[2,1,128,128]{3,2,1,0:T(8,128)S(1)},...) while((s32[]{:T(128)}, f32[1,128,128]{2,1,0:T(8,128)S(1)}, ...), condition=%wide.region_4.5_spmd.clone, body=%wide.region_1.4_spmd.clone.sunk | while | flops 337793024 | bytes 6143455 | solution.py:115
  11.0 1.7 fusion.121
  13.3 2.4 dynamic_update_slice.28
  22.4 1.7 fusion.121
  24.7 2.4 dynamic_update_slice.28
  39.1 157.0 %all-reduce.4 = f32[64]{0:T(128)S(1)} all-reduce(f32[64]{0:T(128)S(1)} %fusion.91), channel_id=2, replica_groups=mesh['seq'=64,'head'=16] {'seq'}, use_global_device_ids=true, to_apply=%add.4 | all-reduce | flops 64 | bytes 512
  196.1 132.6 %while.60 = (s32[]{:T(128)}, f32[1,128,128]{2,1,0:T(8,128)S(1)}, s32[]{:T(128)}, f32[64,1]{0,1:T(1,128)S(1)}, f32[64,1,128,128]{3,2,1,0:T(8,128)}, /*index=5*/s32[]{:T(128)}, s32[]{:T(128)}) while((s32[]{:T(128)}, f32[1,128,128]{2,1,0:T(8,128)S(1)}, s32[]{:T(128)}, f32[64,1]{0,1:T(1,128)S(1)}, f32[64,1,128,128]{3,2,1,0:T(8,128)}, ...), condition=%wide.region_10.11_spmd.clone, body=%wide.region_9.10_spmd.clone.sunk | while | flops 65540 | bytes 196725 | solution.py:26
  198.8 1.5 fusion.123
  203.0 1.5 fusion.123
  207.2 1.5 fusion.123
  211.4 1.5 fusion.123
  215.6 1.5 fusion.123
  219.8 1.5 fusion.123
  224.1 1.5 fusion.123
  226.2 1.5 fusion.123
  230.4 1.5 fusion.123
  328.8 414.1 %while.58 = (s32[]{:T(128)}, bf16[8,8,1,128,128]{4,3,1,2,0:T(8,128)(2,1)}, s32[8,8]{1,0:T(8,128)S(1)}, s32[1024]{0:T(1024)S(1)}, f32[1,1024]{1,0:T(1,128)}, /*in...) while((s32[]{:T(128)}, ...), condition=%wide.region_17.18_spmd, body=%wide.region_14.17_spmd.sunk | while | flops 136997552 | bytes 8904945 | solution.py:163
  328.8 15.0 %while.63 = (s32[]{:T(128)}, f32[1,1024]{1,0:T(1,128)}, s32[8,2]{0,1:T(2,128)S(1)}, f32[8,1,512]{2,1,0:T(1,128)S(1)}, s32[]{:T(128)}) while((s32[]{:T(128)}, f32[1,1024]{1,0:T(1,128)}, s32[8,2]{0,1:T(2,128)S(1)}, f32[8,1,512]{2,1,0:T(1,128)S(1)}, s32[]{:T(128)}) %tuple.187), condition=%wide.while_cond.1, body=%wide.while_body.1.sunk | while | flops 2 | bytes 4193 | solution.py:146
  345.9 9.8 %while.64 = (s32[]{:T(128)}, s32[1024]{0:T(1024)S(1)}, s32[8,1]{0,1:T(1,128)S(1)}, s32[8,512]{1,0:T(8,128)S(1)}, s32[]{:T(128)}, /*index=5*/s32[]{:T(128)}) while((s32[]{:T(128)}, s32[1024]{0:T(1024)S(1)}, s32[8,1]{0,1:T(1,128)S(1)}, s32[8,512]{1,0:T(8,128)S(1)}, s32[]{:T(128)}, /*index=5*/s32[]{:T(128)}) %tuple.190), condition=%wide.while_cond, body=%wide.while_body.sunk | while | flops 2 | bytes 8281 | solution.py:147
  358.6 9.4 %while.62 = (s32[]{:T(128)}, bf16[1024,1,128]{2,0,1:T(8,128)(2,1)S(1)}, s32[8,3]{0,1:T(4,128)S(1)}, bf16[8,512,1,128]{3,1,2,0:T(8,128)(2,1)S(1)}, s32[]{:T(128)}) while((s32[]{:T(128)}, bf16[1024,1,128]{2,0,1:T(8,128)(2,1)S(1)}, s32[8,3]{0,1:T(4,128)S(1)}, bf16[8,512,1,128]{3,1,2,0:T(8,128)(2,1)S(1)}, s32[]{:T(128)}) %tuple.209), condition=%wide.while_cond.3, body=%wide.while_body.3.sunk | while | flops 2 | bytes 262249 | solution.py:145
  368.2 9.4 %while.61 = (s32[]{:T(128)}, bf16[1024,1,128]{2,0,1:T(8,128)(2,1)S(1)}, s32[8,3]{0,1:T(4,128)S(1)}, bf16[8,512,1,128]{3,1,2,0:T(8,128)(2,1)S(1)}, s32[]{:T(128)}) while((s32[]{:T(128)}, bf16[1024,1,128]{2,0,1:T(8,128)(2,1)S(1)}, s32[8,3]{0,1:T(4,128)S(1)}, bf16[8,512,1,128]{3,1,2,0:T(8,128)(2,1)S(1)}, s32[]{:T(128)}) %tuple.210), condition=%wide.while_cond.2, body=%wide.while_body.2.sunk | while | flops 2 | bytes 262249 | solution.py:144
  378.3 2.3 fusion.111
  380.6 15.0 %while.63 = (s32[]{:T(128)}, f32[1,1024]{1,0:T(1,128)}, s32[8,2]{0,1:T(2,128)S(1)}, f32[8,1,512]{2,1,0:T(1,128)S(1)}, s32[]{:T(128)}) while((s32[]{:T(128)}, f32[1,1024]{1,0:T(1,128)}, s32[8,2]{0,1:T(2,128)S(1)}, f32[8,1,512]{2,1,0:T(1,128)S(1)}, s32[]{:T(128)}) %tuple.187), condition=%wide.while_cond.1, body=%wide.while_body.1.sunk | while | flops 2 | bytes 4193 | solution.py:146
  397.7 9.8 %while.64 = (s32[]{:T(128)}, s32[1024]{0:T(1024)S(1)}, s32[8,1]{0,1:T(1,128)S(1)}, s32[8,512]{1,0:T(8,128)S(1)}, s32[]{:T(128)}, /*index=5*/s32[]{:T(128)}) while((s32[]{:T(128)}, s32[1024]{0:T(1024)S(1)}, s32[8,1]{0,1:T(1,128)S(1)}, s32[8,512]{1,0:T(8,128)S(1)}, s32[]{:T(128)}, /*index=5*/s32[]{:T(128)}) %tuple.190), condition=%wide.while_cond, body=%wide.while_body.sunk | while | flops 2 | bytes 8281 | solution.py:147
  410.4 9.4 %while.62 = (s32[]{:T(128)}, bf16[1024,1,128]{2,0,1:T(8,128)(2,1)S(1)}, s32[8,3]{0,1:T(4,128)S(1)}, bf16[8,512,1,128]{3,1,2,0:T(8,128)(2,1)S(1)}, s32[]{:T(128)}) while((s32[]{:T(128)}, bf16[1024,1,128]{2,0,1:T(8,128)(2,1)S(1)}, s32[8,3]{0,1:T(4,128)S(1)}, bf16[8,512,1,128]{3,1,2,0:T(8,128)(2,1)S(1)}, s32[]{:T(128)}) %tuple.209), condition=%wide.while_cond.3, body=%wide.while_body.3.sunk | while | flops 2 | bytes 262249 | solution.py:145
  420.0 9.4 %while.61 = (s32[]{:T(128)}, bf16[1024,1,128]{2,0,1:T(8,128)(2,1)S(1)}, s32[8,3]{0,1:T(4,128)S(1)}, bf16[8,512,1,128]{3,1,2,0:T(8,128)(2,1)S(1)}, s32[]{:T(128)}) while((s32[]{:T(128)}, bf16[1024,1,128]{2,0,1:T(8,128)(2,1)S(1)}, s32[8,3]{0,1:T(4,128)S(1)}, bf16[8,512,1,128]{3,1,2,0:T(8,128)(2,1)S(1)}, s32[]{:T(128)}) %tuple.210), condition=%wide.while_cond.2, body=%wide.while_body.2.sunk | while | flops 2 | bytes 262249 | solution.py:144
  430.0 2.3 fusion.111
  432.4 15.0 %while.63 = (s32[]{:T(128)}, f32[1,1024]{1,0:T(1,128)}, s32[8,2]{0,1:T(2,128)S(1)}, f32[8,1,512]{2,1,0:T(1,128)S(1)}, s32[]{:T(128)}) while((s32[]{:T(128)}, f32[1,1024]{1,0:T(1,128)}, s32[8,2]{0,1:T(2,128)S(1)}, f32[8,1,512]{2,1,0:T(1,128)S(1)}, s32[]{:T(128)}) %tuple.187), condition=%wide.while_cond.1, body=%wide.while_body.1.sunk | while | flops 2 | bytes 4193 | solution.py:146
  449.4 9.8 %while.64 = (s32[]{:T(128)}, s32[1024]{0:T(1024)S(1)}, s32[8,1]{0,1:T(1,128)S(1)}, s32[8,512]{1,0:T(8,128)S(1)}, s32[]{:T(128)}, /*index=5*/s32[]{:T(128)}) while((s32[]{:T(128)}, s32[1024]{0:T(1024)S(1)}, s32[8,1]{0,1:T(1,128)S(1)}, s32[8,512]{1,0:T(8,128)S(1)}, s32[]{:T(128)}, /*index=5*/s32[]{:T(128)}) %tuple.190), condition=%wide.while_cond, body=%wide.while_body.sunk | while | flops 2 | bytes 8281 | solution.py:147
  462.1 9.4 %while.62 = (s32[]{:T(128)}, bf16[1024,1,128]{2,0,1:T(8,128)(2,1)S(1)}, s32[8,3]{0,1:T(4,128)S(1)}, bf16[8,512,1,128]{3,1,2,0:T(8,128)(2,1)S(1)}, s32[]{:T(128)}) while((s32[]{:T(128)}, bf16[1024,1,128]{2,0,1:T(8,128)(2,1)S(1)}, s32[8,3]{0,1:T(4,128)S(1)}, bf16[8,512,1,128]{3,1,2,0:T(8,128)(2,1)S(1)}, s32[]{:T(128)}) %tuple.209), condition=%wide.while_cond.3, body=%wide.while_body.3.sunk | while | flops 2 | bytes 262249 | solution.py:145
  471.7 9.4 %while.61 = (s32[]{:T(128)}, bf16[1024,1,128]{2,0,1:T(8,128)(2,1)S(1)}, s32[8,3]{0,1:T(4,128)S(1)}, bf16[8,512,1,128]{3,1,2,0:T(8,128)(2,1)S(1)}, s32[]{:T(128)}) while((s32[]{:T(128)}, bf16[1024,1,128]{2,0,1:T(8,128)(2,1)S(1)}, s32[8,3]{0,1:T(4,128)S(1)}, bf16[8,512,1,128]{3,1,2,0:T(8,128)(2,1)S(1)}, s32[]{:T(128)}) %tuple.210), condition=%wide.while_cond.2, body=%wide.while_body.2.sunk | while | flops 2 | bytes 262249 | solution.py:144
  481.8 2.3 fusion.111
  484.1 15.0 %while.63 = (s32[]{:T(128)}, f32[1,1024]{1,0:T(1,128)}, s32[8,2]{0,1:T(2,128)S(1)}, f32[8,1,512]{2,1,0:T(1,128)S(1)}, s32[]{:T(128)}) while((s32[]{:T(128)}, f32[1,1024]{1,0:T(1,128)}, s32[8,2]{0,1:T(2,128)S(1)}, f32[8,1,512]{2,1,0:T(1,128)S(1)}, s32[]{:T(128)}) %tuple.187), condition=%wide.while_cond.1, body=%wide.while_body.1.sunk | while | flops 2 | bytes 4193 | solution.py:146
  501.2 9.8 %while.64 = (s32[]{:T(128)}, s32[1024]{0:T(1024)S(1)}, s32[8,1]{0,1:T(1,128)S(1)}, s32[8,512]{1,0:T(8,128)S(1)}, s32[]{:T(128)}, /*index=5*/s32[]{:T(128)}) while((s32[]{:T(128)}, s32[1024]{0:T(1024)S(1)}, s32[8,1]{0,1:T(1,128)S(1)}, s32[8,512]{1,0:T(8,128)S(1)}, s32[]{:T(128)}, /*index=5*/s32[]{:T(128)}) %tuple.190), condition=%wide.while_cond, body=%wide.while_body.sunk | while | flops 2 | bytes 8281 | solution.py:147
  513.9 9.4 %while.62 = (s32[]{:T(128)}, bf16[1024,1,128]{2,0,1:T(8,128)(2,1)S(1)}, s32[8,3]{0,1:T(4,128)S(1)}, bf16[8,512,1,128]{3,1,2,0:T(8,128)(2,1)S(1)}, s32[]{:T(128)}) while((s32[]{:T(128)}, bf16[1024,1,128]{2,0,1:T(8,128)(2,1)S(1)}, s32[8,3]{0,1:T(4,128)S(1)}, bf16[8,512,1,128]{3,1,2,0:T(8,128)(2,1)S(1)}, s32[]{:T(128)}) %tuple.209), condition=%wide.while_cond.3, body=%wide.while_body.3.sunk | while | flops 2 | bytes 262249 | solution.py:145
  523.5 9.4 %while.61 = (s32[]{:T(128)}, bf16[1024,1,128]{2,0,1:T(8,128)(2,1)S(1)}, s32[8,3]{0,1:T(4,128)S(1)}, bf16[8,512,1,128]{3,1,2,0:T(8,128)(2,1)S(1)}, s32[]{:T(128)}) while((s32[]{:T(128)}, bf16[1024,1,128]{2,0,1:T(8,128)(2,1)S(1)}, s32[8,3]{0,1:T(4,128)S(1)}, bf16[8,512,1,128]{3,1,2,0:T(8,128)(2,1)S(1)}, s32[]{:T(128)}) %tuple.210), condition=%wide.while_cond.2, body=%wide.while_body.2.sunk | while | flops 2 | bytes 262249 | solution.py:144
  533.5 2.3 fusion.111
  535.9 15.0 %while.63 = (s32[]{:T(128)}, f32[1,1024]{1,0:T(1,128)}, s32[8,2]{0,1:T(2,128)S(1)}, f32[8,1,512]{2,1,0:T(1,128)S(1)}, s32[]{:T(128)}) while((s32[]{:T(128)}, f32[1,1024]{1,0:T(1,128)}, s32[8,2]{0,1:T(2,128)S(1)}, f32[8,1,512]{2,1,0:T(1,128)S(1)}, s32[]{:T(128)}) %tuple.187), condition=%wide.while_cond.1, body=%wide.while_body.1.sunk | while | flops 2 | bytes 4193 | solution.py:146
  552.9 9.8 %while.64 = (s32[]{:T(128)}, s32[1024]{0:T(1024)S(1)}, s32[8,1]{0,1:T(1,128)S(1)}, s32[8,512]{1,0:T(8,128)S(1)}, s32[]{:T(128)}, /*index=5*/s32[]{:T(128)}) while((s32[]{:T(128)}, s32[1024]{0:T(1024)S(1)}, s32[8,1]{0,1:T(1,128)S(1)}, s32[8,512]{1,0:T(8,128)S(1)}, s32[]{:T(128)}, /*index=5*/s32[]{:T(128)}) %tuple.190), condition=%wide.while_cond, body=%wide.while_body.sunk | while | flops 2 | bytes 8281 | solution.py:147
  565.6 9.4 %while.62 = (s32[]{:T(128)}, bf16[1024,1,128]{2,0,1:T(8,128)(2,1)S(1)}, s32[8,3]{0,1:T(4,128)S(1)}, bf16[8,512,1,128]{3,1,2,0:T(8,128)(2,1)S(1)}, s32[]{:T(128)}) while((s32[]{:T(128)}, bf16[1024,1,128]{2,0,1:T(8,128)(2,1)S(1)}, s32[8,3]{0,1:T(4,128)S(1)}, bf16[8,512,1,128]{3,1,2,0:T(8,128)(2,1)S(1)}, s32[]{:T(128)}) %tuple.209), condition=%wide.while_cond.3, body=%wide.while_body.3.sunk | while | flops 2 | bytes 262249 | solution.py:145
  575.2 9.4 %while.61 = (s32[]{:T(128)}, bf16[1024,1,128]{2,0,1:T(8,128)(2,1)S(1)}, s32[8,3]{0,1:T(4,128)S(1)}, bf16[8,512,1,128]{3,1,2,0:T(8,128)(2,1)S(1)}, s32[]{:T(128)}) while((s32[]{:T(128)}, bf16[1024,1,128]{2,0,1:T(8,128)(2,1)S(1)}, s32[8,3]{0,1:T(4,128)S(1)}, bf16[8,512,1,128]{3,1,2,0:T(8,128)(2,1)S(1)}, s32[]{:T(128)}) %tuple.210), condition=%wide.while_cond.2, body=%wide.while_body.2.sunk | while | flops 2 | bytes 262249 | solution.py:144
  585.3 2.3 fusion.111
  587.6 15.0 %while.63 = (s32[]{:T(128)}, f32[1,1024]{1,0:T(1,128)}, s32[8,2]{0,1:T(2,128)S(1)}, f32[8,1,512]{2,1,0:T(1,128)S(1)}, s32[]{:T(128)}) while((s32[]{:T(128)}, f32[1,1024]{1,0:T(1,128)}, s32[8,2]{0,1:T(2,128)S(1)}, f32[8,1,512]{2,1,0:T(1,128)S(1)}, s32[]{:T(128)}) %tuple.187), condition=%wide.while_cond.1, body=%wide.while_body.1.sunk | while | flops 2 | bytes 4193 | solution.py:146
  604.7 9.8 %while.64 = (s32[]{:T(128)}, s32[1024]{0:T(1024)S(1)}, s32[8,1]{0,1:T(1,128)S(1)}, s32[8,512]{1,0:T(8,128)S(1)}, s32[]{:T(128)}, /*index=5*/s32[]{:T(128)}) while((s32[]{:T(128)}, s32[1024]{0:T(1024)S(1)}, s32[8,1]{0,1:T(1,128)S(1)}, s32[8,512]{1,0:T(8,128)S(1)}, s32[]{:T(128)}, /*index=5*/s32[]{:T(128)}) %tuple.190), condition=%wide.while_cond, body=%wide.while_body.sunk | while | flops 2 | bytes 8281 | solution.py:147
  617.4 9.4 %while.62 = (s32[]{:T(128)}, bf16[1024,1,128]{2,0,1:T(8,128)(2,1)S(1)}, s32[8,3]{0,1:T(4,128)S(1)}, bf16[8,512,1,128]{3,1,2,0:T(8,128)(2,1)S(1)}, s32[]{:T(128)}) while((s32[]{:T(128)}, bf16[1024,1,128]{2,0,1:T(8,128)(2,1)S(1)}, s32[8,3]{0,1:T(4,128)S(1)}, bf16[8,512,1,128]{3,1,2,0:T(8,128)(2,1)S(1)}, s32[]{:T(128)}) %tuple.209), condition=%wide.while_cond.3, body=%wide.while_body.3.sunk | while | flops 2 | bytes 262249 | solution.py:145
  627.0 9.4 %while.61 = (s32[]{:T(128)}, bf16[1024,1,128]{2,0,1:T(8,128)(2,1)S(1)}, s32[8,3]{0,1:T(4,128)S(1)}, bf16[8,512,1,128]{3,1,2,0:T(8,128)(2,1)S(1)}, s32[]{:T(128)}) while((s32[]{:T(128)}, bf16[1024,1,128]{2,0,1:T(8,128)(2,1)S(1)}, s32[8,3]{0,1:T(4,128)S(1)}, bf16[8,512,1,128]{3,1,2,0:T(8,128)(2,1)S(1)}, s32[]{:T(128)}) %tuple.210), condition=%wide.while_cond.2, body=%wide.while_body.2.sunk | while | flops 2 | bytes 262249 | solution.py:144
  637.0 2.3 fusion.111
  639.4 15.0 %while.63 = (s32[]{:T(128)}, f32[1,1024]{1,0:T(1,128)}, s32[8,2]{0,1:T(2,128)S(1)}, f32[8,1,512]{2,1,0:T(1,128)S(1)}, s32[]{:T(128)}) while((s32[]{:T(128)}, f32[1,1024]{1,0:T(1,128)}, s32[8,2]{0,1:T(2,128)S(1)}, f32[8,1,512]{2,1,0:T(1,128)S(1)}, s32[]{:T(128)}) %tuple.187), condition=%wide.while_cond.1, body=%wide.while_body.1.sunk | while | flops 2 | bytes 4193 | solution.py:146
  656.4 9.8 %while.64 = (s32[]{:T(128)}, s32[1024]{0:T(1024)S(1)}, s32[8,1]{0,1:T(1,128)S(1)}, s32[8,512]{1,0:T(8,128)S(1)}, s32[]{:T(128)}, /*index=5*/s32[]{:T(128)}) while((s32[]{:T(128)}, s32[1024]{0:T(1024)S(1)}, s32[8,1]{0,1:T(1,128)S(1)}, s32[8,512]{1,0:T(8,128)S(1)}, s32[]{:T(128)}, /*index=5*/s32[]{:T(128)}) %tuple.190), condition=%wide.while_cond, body=%wide.while_body.sunk | while | flops 2 | bytes 8281 | solution.py:147
  669.1 9.4 %while.62 = (s32[]{:T(128)}, bf16[1024,1,128]{2,0,1:T(8,128)(2,1)S(1)}, s32[8,3]{0,1:T(4,128)S(1)}, bf16[8,512,1,128]{3,1,2,0:T(8,128)(2,1)S(1)}, s32[]{:T(128)}) while((s32[]{:T(128)}, bf16[1024,1,128]{2,0,1:T(8,128)(2,1)S(1)}, s32[8,3]{0,1:T(4,128)S(1)}, bf16[8,512,1,128]{3,1,2,0:T(8,128)(2,1)S(1)}, s32[]{:T(128)}) %tuple.209), condition=%wide.while_cond.3, body=%wide.while_body.3.sunk | while | flops 2 | bytes 262249 | solution.py:145
  678.7 9.4 %while.61 = (s32[]{:T(128)}, bf16[1024,1,128]{2,0,1:T(8,128)(2,1)S(1)}, s32[8,3]{0,1:T(4,128)S(1)}, bf16[8,512,1,128]{3,1,2,0:T(8,128)(2,1)S(1)}, s32[]{:T(128)}) while((s32[]{:T(128)}, bf16[1024,1,128]{2,0,1:T(8,128)(2,1)S(1)}, s32[8,3]{0,1:T(4,128)S(1)}, bf16[8,512,1,128]{3,1,2,0:T(8,128)(2,1)S(1)}, s32[]{:T(128)}) %tuple.210), condition=%wide.while_cond.2, body=%wide.while_body.2.sunk | while | flops 2 | bytes 262249 | solution.py:144
  688.8 2.3 fusion.111
  691.1 15.0 %while.63 = (s32[]{:T(128)}, f32[1,1024]{1,0:T(1,128)}, s32[8,2]{0,1:T(2,128)S(1)}, f32[8,1,512]{2,1,0:T(1,128)S(1)}, s32[]{:T(128)}) while((s32[]{:T(128)}, f32[1,1024]{1,0:T(1,128)}, s32[8,2]{0,1:T(2,128)S(1)}, f32[8,1,512]{2,1,0:T(1,128)S(1)}, s32[]{:T(128)}) %tuple.187), condition=%wide.while_cond.1, body=%wide.while_body.1.sunk | while | flops 2 | bytes 4193 | solution.py:146
  708.2 9.8 %while.64 = (s32[]{:T(128)}, s32[1024]{0:T(1024)S(1)}, s32[8,1]{0,1:T(1,128)S(1)}, s32[8,512]{1,0:T(8,128)S(1)}, s32[]{:T(128)}, /*index=5*/s32[]{:T(128)}) while((s32[]{:T(128)}, s32[1024]{0:T(1024)S(1)}, s32[8,1]{0,1:T(1,128)S(1)}, s32[8,512]{1,0:T(8,128)S(1)}, s32[]{:T(128)}, /*index=5*/s32[]{:T(128)}) %tuple.190), condition=%wide.while_cond, body=%wide.while_body.sunk | while | flops 2 | bytes 8281 | solution.py:147
  720.9 9.4 %while.62 = (s32[]{:T(128)}, bf16[1024,1,128]{2,0,1:T(8,128)(2,1)S(1)}, s32[8,3]{0,1:T(4,128)S(1)}, bf16[8,512,1,128]{3,1,2,0:T(8,128)(2,1)S(1)}, s32[]{:T(128)}) while((s32[]{:T(128)}, bf16[1024,1,128]{2,0,1:T(8,128)(2,1)S(1)}, s32[8,3]{0,1:T(4,128)S(1)}, bf16[8,512,1,128]{3,1,2,0:T(8,128)(2,1)S(1)}, s32[]{:T(128)}) %tuple.209), condition=%wide.while_cond.3, body=%wide.while_body.3.sunk | while | flops 2 | bytes 262249 | solution.py:145
  730.5 9.4 %while.61 = (s32[]{:T(128)}, bf16[1024,1,128]{2,0,1:T(8,128)(2,1)S(1)}, s32[8,3]{0,1:T(4,128)S(1)}, bf16[8,512,1,128]{3,1,2,0:T(8,128)(2,1)S(1)}, s32[]{:T(128)}) while((s32[]{:T(128)}, bf16[1024,1,128]{2,0,1:T(8,128)(2,1)S(1)}, s32[8,3]{0,1:T(4,128)S(1)}, bf16[8,512,1,128]{3,1,2,0:T(8,128)(2,1)S(1)}, s32[]{:T(128)}) %tuple.210), condition=%wide.while_cond.2, body=%wide.while_body.2.sunk | while | flops 2 | bytes 262249 | solution.py:144
  740.6 2.3 fusion.111
  742.8 3.3 convert_bitcast_fusion.1
  746.2 2.7 copy.81
  748.8 6.8 all-to-all-start
  759.9 21.1 %psum.7 = f32[1024]{0:T(1024)S(1)} all-reduce(f32[1024]{0:T(1024)S(1)} %get-tuple-element.647), channel_id=1, replica_groups=mesh['seq'=64,'head'=16] {'head'}, use_global_device_ids=true, to_apply=%region_12.13 | all-reduce | flops 1024 | bytes 8192 | tf_op jit(solution)/shard_map/psum | solution.py:136
  783.0 65.2 %all-to-all-done = bf16[64,1,128,128]{3,2,1,0:T(8,128)(2,1)S(1)} async-done(((bf16[64,1,128,128]{3,2,1,0:T(8,128)(2,1)}), bf16[64,1,128,128]{3,2,1,0:T(8,128)(2,1)S(1)}, u32[]{:S(2)}, u32[]{:S(2)}) %all-to-all-start) | async-done | bytes 2097184 | tf_op jit(solution)/shard_map/all_to_all | solution.py:171
  848.2 1.7 convert_bitcast_fusion
  849.9 2.7 copy.84
  (1202 shorter events, 534.1 us)
Async XLA Ops:
  7.2 188.9 %all-gather.4.cloned.1.call-start = ((), (), s32[]{:S(2)}) async-start(), calls=%async_computation.1 | async-start | bytes 4259840 | tf_op jit(solution)/shard_map/all_gather | solution.py:17
  9.4 24.2 %copy-start.8 = (s32[64]{0:T(128)S(1)}, s32[64]{0:T(128)}, u32[]{:S(2)}) copy-start(s32[64]{0:T(128)} %param.18) | copy-start | bytes 772
  9.4 186.6 %copy-start.7 = (s32[4096]{0:T(1024)S(1)}, s32[4096]{0:T(1024)}, u32[]{:S(2)}) copy-start(s32[4096]{0:T(1024)} %param.19) | copy-start | bytes 49156
  9.4 3.3 copy-start.4
  11.0 8.6 copy-start
  11.0 8.6 copy-start.2
  20.8 3.3 copy-start.4
  22.4 8.6 copy-start
  22.4 8.6 copy-start.2
  32.2 296.6 %copy-start.6 = (f32[2,512,1,128]{1,0,3,2:T(2,128)}, f32[2,512,1,128]{1,0,3,2:T(2,128)S(1)}, u32[]{:S(2)}) copy-start(f32[2,512,1,128]{1,0,3,2:T(2,128)S(1)} %get-tuple-element.378) | copy-start | bytes 1572868
  343.8 14.8 %copy-start.3 = (bf16[1024,1,128]{2,0,1:T(8,128)(2,1)S(1)}, bf16[1024,1,128]{2,0,1:T(8,128)(2,1)}, u32[]{:S(2)}) copy-start(bf16[1024,1,128]{2,0,1:T(8,128)(2,1)} %get-tuple-element.1145) | copy-start | bytes 786436 | tf_op jit(solution)/shard_map/while
  357.7 10.5 %copy-start.1 = (bf16[1024,1,128]{2,0,1:T(8,128)(2,1)S(1)}, bf16[1024,1,128]{2,0,1:T(8,128)(2,1)}, u32[]{:S(2)}) copy-start(bf16[1024,1,128]{2,0,1:T(8,128)(2,1)} %get-tuple-element.1144) | copy-start | bytes 786436 | tf_op jit(solution)/shard_map/while
  395.6 14.8 %copy-start.3 = (bf16[1024,1,128]{2,0,1:T(8,128)(2,1)S(1)}, bf16[1024,1,128]{2,0,1:T(8,128)(2,1)}, u32[]{:S(2)}) copy-start(bf16[1024,1,128]{2,0,1:T(8,128)(2,1)} %get-tuple-element.1145) | copy-start | bytes 786436 | tf_op jit(solution)/shard_map/while
  409.4 10.5 %copy-start.1 = (bf16[1024,1,128]{2,0,1:T(8,128)(2,1)S(1)}, bf16[1024,1,128]{2,0,1:T(8,128)(2,1)}, u32[]{:S(2)}) copy-start(bf16[1024,1,128]{2,0,1:T(8,128)(2,1)} %get-tuple-element.1144) | copy-start | bytes 786436 | tf_op jit(solution)/shard_map/while
  447.4 14.8 %copy-start.3 = (bf16[1024,1,128]{2,0,1:T(8,128)(2,1)S(1)}, bf16[1024,1,128]{2,0,1:T(8,128)(2,1)}, u32[]{:S(2)}) copy-start(bf16[1024,1,128]{2,0,1:T(8,128)(2,1)} %get-tuple-element.1145) | copy-start | bytes 786436 | tf_op jit(solution)/shard_map/while
  461.2 10.5 %copy-start.1 = (bf16[1024,1,128]{2,0,1:T(8,128)(2,1)S(1)}, bf16[1024,1,128]{2,0,1:T(8,128)(2,1)}, u32[]{:S(2)}) copy-start(bf16[1024,1,128]{2,0,1:T(8,128)(2,1)} %get-tuple-element.1144) | copy-start | bytes 786436 | tf_op jit(solution)/shard_map/while
  499.1 14.8 %copy-start.3 = (bf16[1024,1,128]{2,0,1:T(8,128)(2,1)S(1)}, bf16[1024,1,128]{2,0,1:T(8,128)(2,1)}, u32[]{:S(2)}) copy-start(bf16[1024,1,128]{2,0,1:T(8,128)(2,1)} %get-tuple-element.1145) | copy-start | bytes 786436 | tf_op jit(solution)/shard_map/while
  512.9 10.5 %copy-start.1 = (bf16[1024,1,128]{2,0,1:T(8,128)(2,1)S(1)}, bf16[1024,1,128]{2,0,1:T(8,128)(2,1)}, u32[]{:S(2)}) copy-start(bf16[1024,1,128]{2,0,1:T(8,128)(2,1)} %get-tuple-element.1144) | copy-start | bytes 786436 | tf_op jit(solution)/shard_map/while
  550.8 14.8 %copy-start.3 = (bf16[1024,1,128]{2,0,1:T(8,128)(2,1)S(1)}, bf16[1024,1,128]{2,0,1:T(8,128)(2,1)}, u32[]{:S(2)}) copy-start(bf16[1024,1,128]{2,0,1:T(8,128)(2,1)} %get-tuple-element.1145) | copy-start | bytes 786436 | tf_op jit(solution)/shard_map/while
  564.7 10.5 %copy-start.1 = (bf16[1024,1,128]{2,0,1:T(8,128)(2,1)S(1)}, bf16[1024,1,128]{2,0,1:T(8,128)(2,1)}, u32[]{:S(2)}) copy-start(bf16[1024,1,128]{2,0,1:T(8,128)(2,1)} %get-tuple-element.1144) | copy-start | bytes 786436 | tf_op jit(solution)/shard_map/while
  602.6 14.8 %copy-start.3 = (bf16[1024,1,128]{2,0,1:T(8,128)(2,1)S(1)}, bf16[1024,1,128]{2,0,1:T(8,128)(2,1)}, u32[]{:S(2)}) copy-start(bf16[1024,1,128]{2,0,1:T(8,128)(2,1)} %get-tuple-element.1145) | copy-start | bytes 786436 | tf_op jit(solution)/shard_map/while
  616.4 10.5 %copy-start.1 = (bf16[1024,1,128]{2,0,1:T(8,128)(2,1)S(1)}, bf16[1024,1,128]{2,0,1:T(8,128)(2,1)}, u32[]{:S(2)}) copy-start(bf16[1024,1,128]{2,0,1:T(8,128)(2,1)} %get-tuple-element.1144) | copy-start | bytes 786436 | tf_op jit(solution)/shard_map/while
  654.4 14.8 %copy-start.3 = (bf16[1024,1,128]{2,0,1:T(8,128)(2,1)S(1)}, bf16[1024,1,128]{2,0,1:T(8,128)(2,1)}, u32[]{:S(2)}) copy-start(bf16[1024,1,128]{2,0,1:T(8,128)(2,1)} %get-tuple-element.1145) | copy-start | bytes 786436 | tf_op jit(solution)/shard_map/while
  668.2 10.5 %copy-start.1 = (bf16[1024,1,128]{2,0,1:T(8,128)(2,1)S(1)}, bf16[1024,1,128]{2,0,1:T(8,128)(2,1)}, u32[]{:S(2)}) copy-start(bf16[1024,1,128]{2,0,1:T(8,128)(2,1)} %get-tuple-element.1144) | copy-start | bytes 786436 | tf_op jit(solution)/shard_map/while
  706.1 14.8 %copy-start.3 = (bf16[1024,1,128]{2,0,1:T(8,128)(2,1)S(1)}, bf16[1024,1,128]{2,0,1:T(8,128)(2,1)}, u32[]{:S(2)}) copy-start(bf16[1024,1,128]{2,0,1:T(8,128)(2,1)} %get-tuple-element.1145) | copy-start | bytes 786436 | tf_op jit(solution)/shard_map/while
  720.0 10.5 %copy-start.1 = (bf16[1024,1,128]{2,0,1:T(8,128)(2,1)S(1)}, bf16[1024,1,128]{2,0,1:T(8,128)(2,1)}, u32[]{:S(2)}) copy-start(bf16[1024,1,128]{2,0,1:T(8,128)(2,1)} %get-tuple-element.1144) | copy-start | bytes 786436 | tf_op jit(solution)/shard_map/while
  748.8 9.8 %copy-start.5 = (bf16[2,512,1,128]{3,1,2,0:T(8,128)(2,1)S(1)}, bf16[2,512,1,128]{3,1,2,0:T(8,128)(2,1)}, u32[]{:S(2)}) copy-start(bf16[2,512,1,128]{3,1,2,0:T(8,128)(2,1)} %get-tuple-element.1168) | copy-start | bytes 786436
  748.8 99.4 %all-to-all-start = ((bf16[64,1,128,128]{3,2,1,0:T(8,128)(2,1)}), bf16[64,1,128,128]{3,2,1,0:T(8,128)(2,1)S(1)}, u32[]{:S(2)}, u32[]{:S(2)}) async-start(bf16[64,1,128,128]{3,2,1,0:T(8,128)(2,1)} %copy.81), calls=%async_computation | async-start | bytes 4194304 | tf_op jit(solution)/shard_map/all_to_all | solution.py:171
  755.7 25.3 %copy-start.9 = (f32[1,128]{1,0:T(1,128)S(1)}, f32[1,128]{1,0:T(1,128)}, u32[]{:S(2)}) copy-start(f32[1,128]{1,0:T(1,128)} %param.17) | copy-start | bytes 1540
Sparse Core Ops, SparseCore 0:
  33.7 160.1 all-gather.3
where the time goes:
time: 868 us; the launch traced here: 859 us
  local copies, waits for them, and re-layouts  437 us (50%)
  blocking collectives  178 us (21%)
  other arithmetic  118 us (14%)
  waiting for transfers between devices  65.2 us (8%)
  matrix products  29.6 us (3%)
  between operations  14.9 us (2%)
  loops' own time  10.1 us (1%)
    gather x768, local copies, waits for them, and re-layouts  346 us
    unnamed x1, blocking collectives  157 us
    select_n x63, other arithmetic, turn(): jnp.where(position < mine, new, old)  94.8 us
    all_to_all x1, waiting for transfers between devices, shards(): lax.all_to_all(outgoing, 'seq', split_axis=0, concat_axis=0, tiled=True)  65.2 us
    dynamic_slice x63, local copies, waits for them, and re-layouts, turn(): longer = join(total, jax.tree.map(lambda part: part[position], pieces))  36.8 us
    psum x1, blocking collectives, shards(): squares = lax.psum(jnp.sum(mixed_out * mixed_out, axis=(1, 2)), 'head')  21.1 us
    dot_general x8, matrix products, end_state(): jnp.einsum('shd,shv->hdv', decayed, value_block, preferred_element_type=j...  18.2 us
  transfers between devices with their start and end apart: 2, of which 1 were waited for; matrix products, arithmetic and copies ran while one was open for 1% of the time, Pallas kernels for 0%

commit v1 on v0

v1 whole, which is shorter than its diff:
```python
import functools

import jax
import jax.numpy as jnp
from jax import lax
from jax.experimental import pallas as pl
from jax.experimental.pallas import tpu as pltpu
from jax.sharding import PartitionSpec as P

EPS = 1e-05
RING = 4
TILE = 128
MESH = pl.DeviceIdType.MESH
F32 = jnp.float32
BF16 = jnp.bfloat16


def row_to_col(row):
    n = row.shape[1]
    eye = lax.broadcasted_iota(jnp.int32, (n, n), 0) == lax.broadcasted_iota(jnp.int32, (n, n), 1)
    return jnp.sum(jnp.where(eye, jnp.broadcast_to(row, (n, n)), 0.0), axis=1, keepdims=True)


def spread_col(row):
    n = row.shape[1]
    return jnp.transpose(jnp.broadcast_to(row, (n, n)))


def running_sum(gates):
    rows, lanes = gates.shape
    lane = lax.broadcasted_iota(jnp.int32, gates.shape, 1)
    sub = lax.broadcasted_iota(jnp.int32, gates.shape, 0)
    total = gates
    step = 1
    while step < lanes:
        total = total + jnp.where(lane >= step, pltpu.roll(total, step, 1), 0.0)
        step *= 2
    last = jnp.broadcast_to(total[:, lanes - 1 :], gates.shape)
    before = jnp.where(sub >= 1, pltpu.roll(last, 1, 0), 0.0)
    step = 1
    while step < rows:
        before = before + jnp.where(sub >= step, pltpu.roll(before, step, 0), 0.0)
        step *= 2
    return total + before


def front(
    groups,
    q_ref,
    k_ref,
    v_ref,
    gate_ref,
    ends_ref,
    page_ref,
    slots_ref,
    mixed_ref,
    squares_ref,
    raw_t,
    scaled_t,
    lhs,
    state,
    link,
    x_state,
    x_link,
    z_out,
    z_link_out,
    z_state,
    z_link,
    back_out,
    back_in,
    first_state,
    sem_xs,
    sem_xr,
    sem_xls,
    sem_xlr,
    sem_zs,
    sem_zr,
    sem_zls,
    sem_zlr,
    sem_bs,
    sem_br,
):
    place = lax.axis_index("seq")
    head = lax.axis_index("head")
    z, x = place // RING, place % RING
    tokens, depth = k_ref.shape
    tiles = tokens // TILE
    docs = ends_ref.shape[1]
    owners = slots_ref.shape[0]
    quarter = depth // RING

    barrier = pltpu.get_barrier_semaphore()
    for hop in range(1, RING):
        peer = z * RING + (x + hop) % RING
        pl.semaphore_signal(barrier, inc=1, device_id=(peer, head), device_id_type=MESH)
    for hop in range(1, groups):
        peer = ((z + hop) % groups) * RING + x
        pl.semaphore_signal(barrier, inc=1, device_id=(peer, head), device_id_type=MESH)

    cum = running_sum(gate_ref[...])
    ends = row_to_col(ends_ref[...].astype(F32))
    pages = page_ref[pl.ds(place, 1), :]
    owner = row_to_col((pages >> (owners.bit_length() - 1)).astype(F32))
    used = ends > 0.0
    lane = lax.broadcasted_iota(jnp.int32, (docs, TILE), 1).astype(F32)
    doc = lax.broadcasted_iota(jnp.int32, (docs, TILE), 0).astype(F32)
    cum_row = [cum[t : t + 1, :] for t in range(tiles)]
    total = cum[tiles - 1 :, TILE - 1 :]
    seg_row = []
    at_end = jnp.zeros((docs, 1), F32)
    for t in range(tiles):
        position = lane + float(t * TILE)
        seg_row.append(
            jnp.sum(jnp.where(used & (ends <= position), 1.0, 0.0), axis=0, keepdims=True)
        )
        at_end = at_end + jnp.sum(
            jnp.where(position == ends - 1.0, jnp.broadcast_to(cum_row[t], position.shape), 0.0),
            axis=1,
            keepdims=True,
        )
    own_row, open_row = [], []
    for t in range(tiles):
        inside = (jnp.broadcast_to(seg_row[t], doc.shape) == doc) & used
        done = jnp.sum(jnp.where(inside, 1.0, 0.0), axis=0, keepdims=True)
        stop = jnp.sum(jnp.where(inside, at_end, 0.0), axis=0, keepdims=True)
        owned = jnp.sum(jnp.where(inside, owner, 0.0), axis=0, keepdims=True)
        stop = jnp.where(done > 0.0, stop, total)
        own_row.append(jnp.where(done > 0.0, owned, -1.0))
        open_row.append(jnp.where(done > 0.0, 0.0, 1.0))
        weight = jnp.exp(stop - cum_row[t])
        turned = jnp.transpose(k_ref[pl.ds(t * TILE, TILE), :].astype(F32))
        cols = pl.ds(t * TILE, TILE)
        raw_t[:, cols] = turned.astype(BF16)
        turned = turned * weight
        high = turned.astype(BF16)
        scaled_t[:, cols] = high
        keep = open_row[t]
        low = ((turned - high.astype(F32)) * keep).astype(BF16)
        values = v_ref[pl.ds(t * TILE, TILE), :]
        piece = jnp.dot((high.astype(F32) * keep).astype(BF16), values, preferred_element_type=F32)
        piece = piece + jnp.dot(low, values, preferred_element_type=F32)
        if t == 0:
            state[...] = piece
        else:
            state[...] += piece
    any_ended = jnp.sum(jnp.where(used, 1.0, 0.0), axis=0, keepdims=True)
    through = jnp.where(any_ended > 0.0, 0.0, jnp.exp(total))
    link[0] = jnp.broadcast_to(through, (1, TILE))

    pl.semaphore_wait(barrier, RING + groups - 2)

    def x_copies(hop):
        to = (x + hop) % RING
        device = (z * RING + to, head)
        rows = pl.ds(pl.multiple_of(to * quarter, quarter), quarter)
        return (
            pltpu.make_async_remote_copy(
                state.at[rows], x_state.at[x], sem_xs.at[hop], sem_xr.at[x], device, MESH
            ),
            pltpu.make_async_remote_copy(
                link.at[0], x_link.at[x], sem_xls.at[hop], sem_xlr.at[x], device, MESH
            ),
        )

    for hop in (2, 1, 3):
        for copy in x_copies(hop):
            copy.start()
    mine = pl.ds(pl.multiple_of(x * quarter, quarter), quarter)
    x_state[x] = state[mine, :]
    x_link[x] = link[0]

    for t in range(tiles):
        cum_col = spread_col(cum_row[t])
        seg_col = spread_col(seg_row[t])
        queries = q_ref[pl.ds(t * TILE, TILE), :]
        part = None
        for j in range(t + 1):
            cols = pl.ds(j * TILE, TILE)
            scores = jnp.dot(queries, raw_t[:, cols], preferred_element_type=F32)
            allowed = seg_col == seg_row[j]
            if j == t:
                allowed = allowed & (
                    lax.broadcasted_iota(jnp.int32, (TILE, TILE), 0)
                    >= lax.broadcasted_iota(jnp.int32, (TILE, TILE), 1)
                )
            damping = jnp.exp(jnp.where(allowed, cum_col - cum_row[j], -jnp.inf))
            term = jnp.dot(
                (scores * damping).astype(BF16), v_ref[cols, :], preferred_element_type=F32
            )
            part = term if part is None else part + term
        mixed_ref[pl.ds(t * TILE, TILE), :] = part

    for hop in range(1, RING):
        sender = (x + hop) % RING
        pltpu.make_async_remote_copy(
            x_state.at[sender], x_state.at[sender], sem_xs.at[hop], sem_xr.at[sender], (place, head), MESH
        ).wait_recv()
        pltpu.make_async_remote_copy(
            x_link.at[sender], x_link.at[sender], sem_xls.at[hop], sem_xlr.at[sender], (place, head), MESH
        ).wait_recv()
    group_state, group_link = x_state[0], x_link[0]
    for n in range(1, RING):
        group_state = group_state * x_link[n] + x_state[n]
        group_link = group_link * x_link[n]
    z_out[...] = group_state.astype(BF16)
    z_link_out[0] = group_link

    def z_copies(hop):
        device = ((z + hop) * RING + x, head)
        return (
            pltpu.make_async_remote_copy(
                z_out, z_state.at[z], sem_zs.at[hop], sem_zr.at[z], device, MESH
            ),
            pltpu.make_async_remote_copy(
                z_link_out.at[0], z_link.at[z], sem_zls.at[hop], sem_zlr.at[z], device, MESH
            ),
        )

    for hop in sorted(range(1, groups), key=lambda n: -min(n, groups - n)):

        @pl.when(z + hop < groups)
        def _():
            for copy in z_copies(hop):
                copy.start()

    own_all = jnp.concatenate(own_row, axis=1)
    batch = lhs.shape[0] // depth

    def slot_group(n, carry):
        for b in range(batch):
            number = (n * batch + b).astype(F32)
            mask = jnp.where(own_all == number, 1.0, 0.0).astype(BF16)
            lhs[pl.ds(b * depth, depth), :] = scaled_t[...] * mask
        result = jnp.dot(lhs[...], v_ref[...], preferred_element_type=F32)
        slots_ref[pl.ds(n * batch, batch)] = result.astype(BF16).reshape(
            batch, depth, v_ref.shape[1]
        )
        return carry

    lax.fori_loop(0, owners // batch, slot_group, 0)
    leading = jnp.where((jnp.concatenate(seg_row, axis=1) == 0.0) & (own_all >= 0.0), 1.0, 0.0)
    first_state[...] = jnp.dot(
        scaled_t[...] * leading.astype(BF16), v_ref[...], preferred_element_type=F32
    )

    def z_turn(n, total_state):
        pltpu.make_async_remote_copy(
            z_out, z_state.at[n], sem_zs.at[0], sem_zr.at[n], (place, head), MESH
        ).wait_recv()
        pltpu.make_async_remote_copy(
            z_link_out.at[0], z_link.at[n], sem_zls.at[0], sem_zlr.at[n], (place, head), MESH
        ).wait_recv()
        return total_state * z_link[n] + z_state[n].astype(F32)

    reached = lax.fori_loop(0, z, z_turn, jnp.zeros((quarter, v_ref.shape[1]), F32))
    for n in range(RING):
        back_out[n] = reached
        reached = reached * x_link[n] + x_state[n]

    def back_copy(hop):
        to = (x + hop) % RING
        return pltpu.make_async_remote_copy(
            back_out.at[to],
            back_in.at[x],
            sem_bs.at[hop],
            sem_br.at[x],
            (z * RING + to, head),
            MESH,
        )

    for hop in (2, 1, 3):
        back_copy(hop).start()
    back_in[x] = back_out[x]
    for hop in range(1, RING):
        for copy in x_copies(hop):
            copy.wait_send()
    for hop in range(1, groups):

        @pl.when(z + hop < groups)
        def _():
            for copy in z_copies(hop):
                copy.wait_send()

    for hop in range(1, RING):
        sender = (x + hop) % RING
        pltpu.make_async_remote_copy(
            back_out.at[0], back_in.at[sender], sem_bs.at[hop], sem_br.at[sender], (place, head), MESH
        ).wait_recv()
    for hop in range(1, RING):
        back_copy(hop).wait_send()

    carry = back_in[...].reshape(depth, v_ref.shape[1])
    leads = ends[0:1, :]
    lead_level = at_end[0:1, :]
    lead_owner = jnp.where(leads > 0.0, owner[0:1, :], -1.0)
    lead = (first_state[...] + jnp.exp(lead_level) * carry).astype(BF16)

    def finish(n, none):
        slots_ref[n] = jnp.where(
            jnp.broadcast_to(lead_owner == n.astype(F32), lead.shape), lead, slots_ref[n]
        )
        return none

    lax.fori_loop(0, owners, finish, 0, unroll=4)
    high = carry.astype(BF16)
    low = (carry - high.astype(F32)).astype(BF16)
    for t in range(tiles):
        rows = pl.ds(t * TILE, TILE)
        queries = q_ref[rows, :]
        reach = spread_col(jnp.where(seg_row[t] == 0.0, jnp.exp(cum_row[t]), 0.0))
        brought = jnp.dot(queries, high, preferred_element_type=F32) + jnp.dot(
            queries, low, preferred_element_type=F32
        )
        out = mixed_ref[rows, :] + brought * reach
        mixed_ref[rows, :] = out
        squares_ref[pl.ds(t, 1), :] = jnp.sum(jnp.transpose(out * out), axis=0, keepdims=True)


def norm(count, mixed_ref, squares_ref, gain_ref, page_ref, first_ref, attended_ref, source_ref):
    tiles = squares_ref.shape[0]
    for t in range(tiles):
        rows = pl.ds(t * TILE, TILE)
        scale = spread_col(lax.rsqrt(squares_ref[pl.ds(t, 1), :] / count + EPS))
        attended_ref[rows, :] = (mixed_ref[rows, :] * scale * gain_ref[...]).astype(BF16)
    senders, docs = page_ref.shape
    pages = lax.broadcasted_iota(jnp.int32, (senders, docs), 0) + first_ref[0]

    def look(n, found):
        row = page_ref[pl.ds(n, 1), :]
        return jnp.where(row == pages, n.astype(F32), found)

    found = lax.fori_loop(0, senders, look, jnp.full((senders, docs), -1.0, F32), unroll=4)
    found = jnp.max(found, axis=1, keepdims=True)
    eye = lax.broadcasted_iota(jnp.int32, (senders, senders), 0) == lax.broadcasted_iota(
        jnp.int32, (senders, senders), 1
    )
    source_ref[...] = jnp.sum(
        jnp.where(eye, jnp.broadcast_to(found, (senders, senders)), 0.0), axis=0, keepdims=True
    ).astype(jnp.int32)


def settle(source_ref, incoming_ref, cache_ref, blank, sem):
    blank[...] = jnp.zeros_like(blank)
    pages = cache_ref.shape[0]

    def begin(n, none):
        source = source_ref[0, n]

        @pl.when(source >= 0)
        def _():
            pltpu.make_async_copy(incoming_ref.at[source], cache_ref.at[n], sem).start()

        @pl.when(source < 0)
        def _():
            pltpu.make_async_copy(blank, cache_ref.at[n], sem).start()

        return none

    lax.fori_loop(0, pages, begin, 0)
    pltpu.make_async_copy(incoming_ref, cache_ref, sem).wait()


VMEM = pl.BlockSpec(memory_space=pltpu.VMEM)
SMEM = pl.BlockSpec(memory_space=pltpu.SMEM)
LIMIT = 48 << 20


def shards(query_rows, key_rows, value_rows, log_gate, norm_gain, doc_ends, doc_page):
    tokens, heads, depth = query_rows.shape
    width = value_rows.shape[2]
    devices = lax.axis_size("seq")
    bounds = doc_ends.shape[0]
    groups = devices // RING
    quarter = depth // RING
    table = doc_page.reshape(devices, bounds)
    dma = pltpu.SemaphoreType.DMA
    slots, mixed, squares = pl.pallas_call(
        functools.partial(front, groups),
        out_shape=(
            jax.ShapeDtypeStruct((devices, depth, width), BF16),
            jax.ShapeDtypeStruct((tokens, width), F32),
            jax.ShapeDtypeStruct((tokens // TILE, TILE), F32),
        ),
        in_specs=[VMEM] * 6,
        out_specs=(VMEM,) * 3,
        scratch_shapes=[
            pltpu.VMEM((depth, tokens), BF16),
            pltpu.VMEM((depth, tokens), BF16),
            pltpu.VMEM((8 * depth, tokens), BF16),
            pltpu.VMEM((depth, width), F32),
            pltpu.VMEM((1, 1, TILE), F32),
            pltpu.VMEM((RING, quarter, width), F32),
            pltpu.VMEM((RING, 1, TILE), F32),
            pltpu.VMEM((quarter, width), BF16),
            pltpu.VMEM((1, 1, TILE), F32),
            pltpu.VMEM((groups, quarter, width), BF16),
            pltpu.VMEM((groups, 1, TILE), F32),
            pltpu.VMEM((RING, quarter, width), F32),
            pltpu.VMEM((RING, quarter, width), F32),
            pltpu.VMEM((depth, width), F32),
            dma((RING,)),
            dma((RING,)),
            dma((RING,)),
            dma((RING,)),
            dma((groups,)),
            dma((groups,)),
            dma((groups,)),
            dma((groups,)),
            dma((RING,)),
            dma((RING,)),
        ],
        compiler_params=pltpu.CompilerParams(
            collective_id=0, has_side_effects=True, vmem_limit_bytes=LIMIT
        ),
        name="front",
    )(
        query_rows.reshape(tokens, depth),
        key_rows.reshape(tokens, depth),
        value_rows.reshape(tokens, width),
        log_gate.reshape(tokens // TILE, TILE),
        doc_ends.reshape(1, bounds),
        table,
    )
    incoming = lax.all_to_all(slots, "seq", split_axis=0, concat_axis=0, tiled=True)
    squares = lax.psum(squares, "head")
    first_page = (lax.axis_index("seq") * devices).astype(jnp.int32).reshape(1)
    attended, source = pl.pallas_call(
        functools.partial(norm, heads * lax.axis_size("head") * width),
        out_shape=(
            jax.ShapeDtypeStruct((tokens, width), BF16),
            jax.ShapeDtypeStruct((1, devices), jnp.int32),
        ),
        in_specs=[VMEM, VMEM, VMEM, VMEM, SMEM],
        out_specs=(VMEM, VMEM),
        name="norm",
    )(mixed, squares, norm_gain, table, first_page)
    cache = pl.pallas_call(
        settle,
        out_shape=jax.ShapeDtypeStruct((devices, depth, width), BF16),
        in_specs=[SMEM, VMEM],
        out_specs=pl.BlockSpec(memory_space=pltpu.HBM),
        scratch_shapes=[pltpu.VMEM((depth, width), BF16), pltpu.SemaphoreType.DMA],
        name="settle",
    )(source, incoming)
    return attended.reshape(tokens, heads, width), cache.reshape(devices, heads, depth, width)


def solution(mesh):
    placed = (
        P("seq", "head", None),
        P("seq", "head", None),
        P("seq", "head", None),
        P("head", "seq"),
        P("head", None),
        P("seq"),
        P(),
    )
    return jax.shard_map(
        shards,
        mesh=mesh,
        in_specs=placed,
        out_specs=(P("seq", "head", None), P("seq", "head", None, None)),
        check_vma=False,
    )
```

time: 868 us -> 158 us (0.18)
  local copies, waits for them, and re-layouts: 437 us -> 7.12 us
  blocking collectives: 178 us -> 21.5 us
  other arithmetic: 118 us -> 0 us
  Pallas kernels: 0 us -> 40.3 us
  matrix products: 29.6 us -> 0 us
  between operations: 14.9 us -> 0.67 us
  loops' own time: 10.1 us -> 0 us
  waiting for transfers between devices: 65.2 us -> 75.3 us
    gather x816 -> x0, local copies, waits for them, and re-layouts: 376 us -> none
    unnamed x1 -> x0, blocking collectives: 157 us -> none
    select_n x76 -> x0, other arithmetic: 96.4 us -> none  [the longest x63 94.8 us: turn(): jnp.where(position < mine, new, old)]
    pallas_call x0 -> x3, Pallas kernels: none -> 40.3 us  [the longest x1 35.2 us: shards(): pl.pallas_call(functools.partial(front, groups), out_shape=(jax.ShapeDtyp...]
    dynamic_slice x65 -> x0, local copies, waits for them, and re-layouts: 38.3 us -> none  [the longest x63 36.8 us: turn(): longer = join(total, jax.tree.map(lambda part: part[position], pieces))]
    dot_general x17 -> x0, matrix products: 29.6 us -> none  [the longest x8 18.2 us: end_state(): jnp.einsum('shd,shv->hdv', decayed, value_block, preferred_element_type=j...]
    another operation x33 -> x0, other arithmetic: 12.3 us -> none
    another operation x35 -> x0, loops' own time: 10.1 us -> none  [the longest x1 4.17 us: shards(): lax.scan(block_step, initial, inputs)]
  transfers between devices with their start and end apart: 2 -> 1, of which waited for: 1 -> 1; matrix products, arithmetic and copies ran while one was open for 1% -> 0% of each run, Pallas kernels for 0% -> 1%
where the time goes in v1:
time: 158 us
  waiting for transfers between devices  75.3 us (48%)
  Pallas kernels  40.3 us (26%)
  blocking collectives  21.5 us (14%)
  starting transfers between devices  12.9 us (8%)
  local copies, waits for them, and re-layouts  7.12 us (5%)
    all_to_all x1, waiting for transfers between devices, shards(): lax.all_to_all(slots, 'seq', split_axis=0, concat_axis=0, tiled=True)  75.3 us
    pallas_call x1, Pallas kernels, shards(): pl.pallas_call(functools.partial(front, groups), out_shape=(jax.ShapeDtyp...  35.2 us
    psum x1, blocking collectives, shards(): squares = lax.psum(squares, 'head')  21.5 us
    all_to_all x1, starting transfers between devices, shards(): lax.all_to_all(slots, 'seq', split_axis=0, concat_axis=0, tiled=True)  12.9 us
    unnamed x16, local copies, waits for them, and re-layouts  6.33 us
  transfers between devices with their start and end apart: 1, of which 1 were waited for; matrix products, arithmetic and copies ran while one was open for 0% of the time, Pallas kernels for 1%

profile of v1, /device:TPU:56, one launch (start us, length us, event | category | flops | bytes accessed | tf_op | source)
XLA Modules:
  0.0 157.7 jit_solution(15401876072678175455)
XLA Ops:
  0.6 0.8 reshape.36.page_ref
  1.4 0.0 copy-start.1
  1.4 0.0 copy-start.2
  1.4 1.0 copy-done.2
  2.4 0.0 copy-start.3
  2.4 0.9 copy-done.3
  3.3 0.0 copy-start.4
  3.3 0.9 copy-done.4
  4.3 0.0 copy-start.5
  4.3 0.7 copy-done.5
  5.0 0.0 copy-start.6
  5.0 0.7 copy-done.6
  5.6 35.2 %front.1 = (bf16[64,128,128]{2,1,0:T(8,128)(2,1)}, f32[1024,128]{1,0:T(8,128)S(1)}, f32[8,128]{1,0:T(8,128)S(1)}) custom-call(bf16[1024,128]{1,0:T(8,128)(2,1)S(1)} %bitcast.10, bf16[1024,128]{1,0:T(8,128)(2,1)S(1)} %bitcast.11, bf16[1024,128]{1,0:T(8,128)(2,1)S(1)} %bitcast.12, f32[8,128]{1,0:T(8,128)S(1)} %bitcast.13, s32[1,64]{1,0:T(1,128)S(1)} %bitcast.14, ...), custom_call_target="tpu_custom_call" | custom-call | tf_op jit(solution)/shard_map/front/pallas_call | solution.py:377
  40.9 0.0 copy-start
  40.9 0.8 copy-done
  41.7 0.0 copy-done.1
  41.7 12.9 %all-to-all-start = ((bf16[64,128,128]{2,1,0:T(8,128)(2,1)}), bf16[64,128,128]{2,1,0:T(8,128)(2,1)S(1)}, u32[]{:S(2)}, u32[]{:S(2)}) async-start(bf16[64,128,128]{2,1,0:T(8,128)(2,1)} %get-tuple-element.11), calls=%async_computation | async-start | bytes 4194304 | tf_op jit(solution)/shard_map/all_to_all | solution.py:424
  54.6 21.5 %psum.7.squares_ref = f32[8,128]{1,0:T(8,128)} all-reduce(f32[8,128]{1,0:T(8,128)S(1)} %get-tuple-element.8), channel_id=1, replica_groups=mesh['seq'=64,'head'=16] {'head'}, use_global_device_ids=true, to_apply=%region_0.0 | all-reduce | flops 1024 | bytes 8192 | tf_op jit(solution)/shard_map/psum | solution.py:425
  76.0 2.1 %norm.1 = (bf16[1024,128]{1,0:T(8,128)(2,1)}, s32[1,64]{1,0:T(1,128)}) custom-call(f32[1024,128]{1,0:T(8,128)} %copy-done, f32[8,128]{1,0:T(8,128)} %psum.7.squares_ref, f32[1,128]{1,0:T(1,128)} %gain_ref.1, s32[64,64]{1,0:T(8,128)} %copy-done.1, s32[1]{0:T(128)} %bitcast.5.first_ref), custom_call_target="tpu_custom_call" | custom-call | tf_op jit(solution)/shard_map/norm/pallas_call | solution.py:427
  78.2 75.3 %all-to-all-done.incoming_ref = bf16[64,128,128]{2,1,0:T(8,128)(2,1)S(1)} async-done(((bf16[64,128,128]{2,1,0:T(8,128)(2,1)}), bf16[64,128,128]{2,1,0:T(8,128)(2,1)S(1)}, u32[]{:S(2)}, u32[]{:S(2)}) %all-to-all-start) | async-done | bytes 2097184 | tf_op jit(solution)/shard_map/all_to_all | solution.py:424
  153.5 0.0 copy-start.7
  153.5 1.3 copy-done.7
  154.8 2.9 %settle.1 = bf16[64,128,128]{2,1,0:T(8,128)(2,1)} custom-call(s32[1,64]{1,0:T(1,128)} %get-tuple-element.10.source_ref, bf16[64,128,128]{2,1,0:T(8,128)(2,1)} %copy-done.7), custom_call_target="tpu_custom_call" | custom-call | tf_op jit(solution)/shard_map/settle/pallas_call | solution.py:437
Async XLA Ops:
  1.4 40.2 %copy-start.1 = (s32[64,64]{1,0:T(8,128)}, s32[64,64]{1,0:T(8,128)S(1)}, u32[]{:S(2)}) copy-start(s32[64,64]{1,0:T(8,128)S(1)} %reshape.36.page_ref) | copy-start | bytes 49156
  1.4 1.0 copy-start.2
  2.4 0.9 copy-start.3
  3.3 0.9 copy-start.4
  4.3 0.7 copy-start.5
  5.0 0.7 copy-start.6
  40.9 0.8 copy-start
  41.7 111.8 %all-to-all-start = ((bf16[64,128,128]{2,1,0:T(8,128)(2,1)}), bf16[64,128,128]{2,1,0:T(8,128)(2,1)S(1)}, u32[]{:S(2)}, u32[]{:S(2)}) async-start(bf16[64,128,128]{2,1,0:T(8,128)(2,1)} %get-tuple-element.11), calls=%async_computation | async-start | bytes 4194304 | tf_op jit(solution)/shard_map/all_to_all | solution.py:424
  153.5 1.3 copy-start.7

commit v2 on v1

v2 whole, which is shorter than its diff:
```python
import functools

import jax
import jax.numpy as jnp
from jax import lax
from jax.experimental import pallas as pl
from jax.experimental.pallas import tpu as pltpu
from jax.sharding import PartitionSpec as P

EPS = 1e-05
RING = 4
TILE = 128
MESH = pl.DeviceIdType.MESH
F32 = jnp.float32
BF16 = jnp.bfloat16


def row_to_col(row):
    n = row.shape[1]
    eye = lax.broadcasted_iota(jnp.int32, (n, n), 0) == lax.broadcasted_iota(jnp.int32, (n, n), 1)
    return jnp.sum(jnp.where(eye, jnp.broadcast_to(row, (n, n)), 0.0), axis=1, keepdims=True)


def spread_col(row):
    n = row.shape[1]
    return jnp.transpose(jnp.broadcast_to(row, (n, n)))


def running_sum(gates):
    rows, lanes = gates.shape
    lane = lax.broadcasted_iota(jnp.int32, gates.shape, 1)
    sub = lax.broadcasted_iota(jnp.int32, gates.shape, 0)
    total = gates
    step = 1
    while step < lanes:
        total = total + jnp.where(lane >= step, pltpu.roll(total, step, 1), 0.0)
        step *= 2
    last = jnp.broadcast_to(total[:, lanes - 1 :], gates.shape)
    before = jnp.where(sub >= 1, pltpu.roll(last, 1, 0), 0.0)
    step = 1
    while step < rows:
        before = before + jnp.where(sub >= step, pltpu.roll(before, step, 0), 0.0)
        step *= 2
    return total + before


def order_of(groups):
    half = groups // 2
    order = [half]
    for hop in range(half - 1, 0, -1):
        order += [hop, -hop]
    return order + [0]


def whole(
    groups,
    heads,
    count,
    q_hbm,
    k_hbm,
    v_hbm,
    gate_hbm,
    ends_hbm,
    table_hbm,
    gain_hbm,
    incoming,
    attended_ref,
    source_ref,
    q_ref,
    k_ref,
    v_ref,
    gate_ref,
    table_ref,
    ends_ref,
    gain_ref,
    slots,
    relay,
    mixed,
    cum_rows,
    seg_rows,
    own_rows,
    squares,
    head_squares,
    raw_t,
    scaled_t,
    lhs,
    state,
    link,
    x_state,
    x_link,
    z_out,
    z_link_out,
    z_state,
    z_link,
    back_out,
    back_in,
    first_state,
    sem_in,
    sem_xs,
    sem_xr,
    sem_xls,
    sem_xlr,
    sem_zs,
    sem_zr,
    sem_zls,
    sem_zlr,
    sem_bs,
    sem_br,
    sem_hs,
    sem_hr,
    sem_os,
    sem_or,
    sem_rs,
    sem_rr,
    sem_fs,
):
    place = lax.axis_index("seq")
    head = lax.axis_index("head")
    z, x = place // RING, place % RING
    tokens, depth = k_ref.shape
    tiles = tokens // TILE
    docs = ends_ref.shape[1]
    owners = slots.shape[0]
    quarter = depth // RING

    loads = [
        pltpu.make_async_copy(source, target, sem_in.at[n])
        for n, (source, target) in enumerate(
            (
                (gate_hbm, gate_ref),
                (table_hbm, table_ref),
                (k_hbm, k_ref),
                (v_hbm, v_ref),
                (q_hbm, q_ref),
                (ends_hbm, ends_ref),
                (gain_hbm, gain_ref),
            )
        )
    ]
    for load in loads:
        load.start()

    barrier = pltpu.get_barrier_semaphore()

    def greet_seq(n, none):
        device = ((place + n) % owners, head)
        pl.semaphore_signal(barrier, inc=1, device_id=device, device_id_type=MESH)
        return none

    def greet_head(n, none):
        device = (place, (head + n) % heads)
        pl.semaphore_signal(barrier, inc=1, device_id=device, device_id_type=MESH)
        return none

    lax.fori_loop(1, owners, greet_seq, 0)
    lax.fori_loop(1, heads, greet_head, 0)

    loads[0].wait()
    loads[1].wait()
    loads[5].wait()
    cum = running_sum(gate_ref[...])
    cum_rows[...] = cum
    ends = row_to_col(ends_ref[...].astype(F32))
    fold = TILE // docs
    pages = jnp.broadcast_to(table_ref[pl.ds(place // fold, 1), :], (8, TILE))
    aligned = pages
    for n in range(1, fold):
        here = jnp.full((8, TILE), place % fold, jnp.int32) == n
        aligned = jnp.where(here, pltpu.roll(pages, TILE - n * docs, 1), aligned)
    owner = row_to_col((aligned[0:1, :docs] >> (owners.bit_length() - 1)).astype(F32))
    used = ends > 0.0
    lane = lax.broadcasted_iota(jnp.int32, (docs, TILE), 1).astype(F32)
    doc = lax.broadcasted_iota(jnp.int32, (docs, TILE), 0).astype(F32)
    cum_row = [cum[t : t + 1, :] for t in range(tiles)]
    total = cum[tiles - 1 :, TILE - 1 :]
    seg_row = []
    at_end = jnp.zeros((docs, 1), F32)
    for t in range(tiles):
        position = lane + float(t * TILE)
        seg_row.append(
            jnp.sum(jnp.where(used & (ends <= position), 1.0, 0.0), axis=0, keepdims=True)
        )
        seg_rows[pl.ds(t, 1), :] = seg_row[t]
        at_end = at_end + jnp.sum(
            jnp.where(position == ends - 1.0, jnp.broadcast_to(cum_row[t], position.shape), 0.0),
            axis=1,
            keepdims=True,
        )
    loads[2].wait()
    loads[3].wait()
    for t in range(tiles):
        inside = (jnp.broadcast_to(seg_row[t], doc.shape) == doc) & used
        done = jnp.sum(jnp.where(inside, 1.0, 0.0), axis=0, keepdims=True)
        stop = jnp.sum(jnp.where(inside, at_end, 0.0), axis=0, keepdims=True)
        owned = jnp.sum(jnp.where(inside, owner, 0.0), axis=0, keepdims=True)
        stop = jnp.where(done > 0.0, stop, total)
        cols = pl.ds(t * TILE, TILE)
        own_rows[:, cols] = jnp.where(done > 0.0, owned, -1.0)
        keep = jnp.where(done > 0.0, 0.0, 1.0)
        weight = jnp.exp(stop - cum_row[t])
        turned = jnp.transpose(k_ref[cols, :].astype(F32))
        raw_t[:, cols] = turned.astype(BF16)
        turned = turned * weight
        high = turned.astype(BF16)
        scaled_t[:, cols] = high
        low = ((turned - high.astype(F32)) * keep).astype(BF16)
        values = v_ref[cols, :]
        piece = jnp.dot((high.astype(F32) * keep).astype(BF16), values, preferred_element_type=F32)
        piece = piece + jnp.dot(low, values, preferred_element_type=F32)
        if t == 0:
            state[...] = piece
        else:
            state[...] += piece
    any_ended = jnp.sum(jnp.where(used, 1.0, 0.0), axis=0, keepdims=True)
    through = jnp.where(any_ended > 0.0, 0.0, jnp.exp(total))
    link[0] = jnp.broadcast_to(through, (1, TILE))

    pl.semaphore_wait(barrier, owners + heads - 2)

    def x_copies(hop):
        to = (x + hop) % RING
        device = (z * RING + to, head)
        rows = pl.ds(pl.multiple_of(to * quarter, quarter), quarter)
        return (
            pltpu.make_async_remote_copy(
                state.at[rows], x_state.at[x], sem_xs.at[hop], sem_xr.at[x], device, MESH
            ),
            pltpu.make_async_remote_copy(
                link.at[0], x_link.at[x], sem_xls.at[hop], sem_xlr.at[x], device, MESH
            ),
        )

    def arrived(target, sem):
        pltpu.make_async_remote_copy(
            target, target, sem_in.at[0], sem, (place, head), MESH
        ).wait_recv()

    for hop in (2, 1, 3):
        for copy in x_copies(hop):
            copy.start()
    mine = pl.ds(pl.multiple_of(x * quarter, quarter), quarter)
    x_state[x] = state[mine, :]
    x_link[x] = link[0]
    for hop in range(1, RING):
        sender = (x + hop) % RING
        arrived(x_state.at[sender], sem_xr.at[sender])
        arrived(x_link.at[sender], sem_xlr.at[sender])
    group_state, group_link = x_state[0], x_link[0]
    for n in range(1, RING):
        group_state = group_state * x_link[n] + x_state[n]
        group_link = group_link * x_link[n]
    z_out[...] = group_state.astype(BF16)
    z_link_out[0] = group_link

    def z_copies(hop):
        device = ((z + hop) * RING + x, head)
        return (
            pltpu.make_async_remote_copy(
                z_out, z_state.at[z], sem_zs.at[hop], sem_zr.at[z], device, MESH
            ),
            pltpu.make_async_remote_copy(
                z_link_out.at[0], z_link.at[z], sem_zls.at[hop], sem_zlr.at[z], device, MESH
            ),
        )

    for hop in sorted(range(1, groups), key=lambda n: -min(n, groups - n)):

        @pl.when(z + hop < groups)
        def _():
            for copy in z_copies(hop):
                copy.start()

    own_all = own_rows[...]
    batch = lhs.shape[0] // depth

    def slot_group(n, carry):
        for b in range(batch):
            number = (n * batch + b).astype(F32)
            mask = jnp.where(own_rows[...] == number, 1.0, 0.0).astype(BF16)
            lhs[pl.ds(b * depth, depth), :] = scaled_t[...] * mask
        result = jnp.dot(lhs[...], v_ref[...], preferred_element_type=F32)
        slots[pl.ds(n * batch, batch)] = result.astype(BF16).reshape(batch, depth, v_ref.shape[1])
        return carry

    lax.fori_loop(0, owners // batch, slot_group, 0)
    leading = jnp.where((jnp.concatenate(seg_row, axis=1) == 0.0) & (own_all >= 0.0), 1.0, 0.0)
    first_state[...] = jnp.dot(
        scaled_t[...] * leading.astype(BF16), v_ref[...], preferred_element_type=F32
    )

    def z_turn(n, total_state):
        arrived(z_state.at[n], sem_zr.at[n])
        arrived(z_link.at[n], sem_zlr.at[n])
        return total_state * z_link[n] + z_state[n].astype(F32)

    reached = lax.fori_loop(0, z, z_turn, jnp.zeros((quarter, v_ref.shape[1]), F32))
    for n in range(RING):
        back_out[n] = reached
        reached = reached * x_link[n] + x_state[n]

    def back_copy(hop):
        to = (x + hop) % RING
        return pltpu.make_async_remote_copy(
            back_out.at[to],
            back_in.at[x],
            sem_bs.at[hop],
            sem_br.at[x],
            (z * RING + to, head),
            MESH,
        )

    for hop in (2, 1, 3):
        back_copy(hop).start()
    back_in[x] = back_out[x]
    for hop in range(1, RING):
        sender = (x + hop) % RING
        arrived(back_in.at[sender], sem_br.at[sender])

    carry = back_in[...].reshape(depth, v_ref.shape[1])
    lead_owner = jnp.where(ends[0:1, :] > 0.0, owner[0:1, :], -1.0)
    lead = (first_state[...] + jnp.exp(at_end[0:1, :]) * carry).astype(BF16)

    half, step_off = groups // 2, groups // 4
    relays = tuple((n, -1 if n % 2 == 0 else 1) for n in range(RING)) if step_off else ()
    order = order_of(groups)
    early = len(order) * 9 // 16

    def target(hop, turn):
        return ((z + hop + groups) % groups) * RING + (x + turn) % RING

    def finish(hop):
        def one(turn, none):
            n = target(hop, turn)
            slots[n] = jnp.where(
                jnp.broadcast_to(lead_owner == n.astype(F32), lead.shape), lead, slots[n]
            )
            return none

        lax.fori_loop(0, RING, one, 0)

    def direct(hop, turn):
        n = target(hop, turn)
        return pltpu.make_async_remote_copy(
            slots.at[n], incoming.at[place], sem_os.at[n], sem_or.at[place], (n, head), MESH
        )

    def first_leg(r):
        turn, way = relays[r]
        via = target(way * step_off, 0)
        return pltpu.make_async_remote_copy(
            slots.at[target(half, turn)],
            relay.at[r],
            sem_rs.at[r],
            sem_rr.at[r],
            (via, head),
            MESH,
        )

    def second_leg(r):
        turn, way = relays[r]
        source = target(-way * step_off, 0)
        return pltpu.make_async_remote_copy(
            relay.at[r],
            incoming.at[source],
            sem_fs.at[r],
            sem_or.at[source],
            (target(way * step_off, turn), head),
            MESH,
        )

    def fire(hop):
        if hop == half and relays:
            for r in range(len(relays)):
                first_leg(r).start()
            return

        def one(turn, none):
            direct(hop, turn).start()
            return none

        lax.fori_loop(1 if hop == 0 else 0, RING, one, 0)

    finish(order[0])
    for n, hop in enumerate(order):
        if n + 1 < len(order):
            finish(order[n + 1])
        if n < early:
            fire(hop)

    incoming[place] = slots[place]
    loads[4].wait()
    loads[6].wait()
    high = carry.astype(BF16)
    low = (carry - high.astype(F32)).astype(BF16)
    later = lax.broadcasted_iota(jnp.int32, (TILE, TILE), 0) - lax.broadcasted_iota(
        jnp.int32, (TILE, TILE), 1
    )

    def attend(t, none):
        rows = pl.ds(pl.multiple_of(t * TILE, TILE), TILE)
        queries = q_ref[rows, :]
        my_cum = cum_rows[pl.ds(t, 1), :]
        my_seg = seg_rows[pl.ds(t, 1), :]
        cum_col = spread_col(my_cum)
        seg_col = spread_col(my_seg)
        reach = spread_col(jnp.where(my_seg == 0.0, jnp.exp(my_cum), 0.0))
        brought = jnp.dot(queries, high, preferred_element_type=F32) + jnp.dot(
            queries, low, preferred_element_type=F32
        )

        def look(j, part):
            cols = pl.ds(pl.multiple_of(j * TILE, TILE), TILE)
            scores = jnp.dot(queries, raw_t[:, cols], preferred_element_type=F32)
            allowed = (seg_col == seg_rows[pl.ds(j, 1), :]) & (later + (t - j) * TILE >= 0)
            damping = jnp.exp(jnp.where(allowed, cum_col - cum_rows[pl.ds(j, 1), :], -jnp.inf))
            return part + jnp.dot(
                (scores * damping).astype(BF16), v_ref[cols, :], preferred_element_type=F32
            )

        out = lax.fori_loop(0, t + 1, look, brought * reach)
        mixed[rows, :] = out
        squares[pl.ds(t, 1), :] = jnp.sum(jnp.transpose(out * out), axis=0, keepdims=True)
        return none

    lax.fori_loop(0, tiles, attend, 0)

    def square_copy(n):
        return pltpu.make_async_remote_copy(
            squares,
            head_squares.at[head],
            sem_hs.at[n],
            sem_hr.at[head],
            (place, (head + n) % heads),
            MESH,
        )

    def send_square(n, none):
        square_copy(n).start()
        return none

    lax.fori_loop(1, heads, send_square, 0)
    head_squares[head] = squares[...]

    for r in range(len(relays)):
        arrived(relay.at[r], sem_rr.at[r])
        second_leg(r).start()
    for hop in order[early:]:
        fire(hop)

    fold_rows = table_ref.shape[0]
    page_lane = lax.broadcasted_iota(jnp.int32, (owners, TILE), 1)
    wanted = lax.broadcasted_iota(jnp.int32, (owners, TILE), 0) + place * owners
    which = (page_lane // docs).astype(F32)

    def search(n, found):
        row = table_ref[pl.ds(n, 1), :]
        return jnp.where(row == wanted, which + (n * fold).astype(F32), found)

    found = lax.fori_loop(0, fold_rows, search, jnp.full((owners, TILE), -1.0, F32))
    found = jnp.max(found, axis=1, keepdims=True)
    eye = lax.broadcasted_iota(jnp.int32, (owners, owners), 0) == lax.broadcasted_iota(
        jnp.int32, (owners, owners), 1
    )
    source_ref[...] = jnp.sum(
        jnp.where(eye, jnp.broadcast_to(found, (owners, owners)), 0.0), axis=0, keepdims=True
    ).astype(jnp.int32)

    def take_square(n, none):
        sender = (head + n) % heads
        arrived(head_squares.at[sender], sem_hr.at[sender])
        return none

    lax.fori_loop(1, heads, take_square, 0)
    energy = head_squares[0]
    for n in range(1, heads):
        energy = energy + head_squares[n]
    cum_rows[...] = lax.rsqrt(energy / count + EPS)

    def normed(t, none):
        rows = pl.ds(pl.multiple_of(t * TILE, TILE), TILE)
        scale = spread_col(cum_rows[pl.ds(t, 1), :])
        attended_ref[rows, :] = (mixed[rows, :] * scale * gain_ref[...]).astype(BF16)
        return none

    lax.fori_loop(0, tiles, normed, 0)

    for hop in range(1, RING):
        for copy in x_copies(hop):
            copy.wait_send()
        back_copy(hop).wait_send()
    for hop in range(1, groups):

        @pl.when(z + hop < groups)
        def _():
            for copy in z_copies(hop):
                copy.wait_send()

    def sent_square(n, none):
        square_copy(n).wait_send()
        return none

    lax.fori_loop(1, heads, sent_square, 0)
    for hop in order:
        if hop == half and relays:
            for r in range(len(relays)):
                first_leg(r).wait_send()
            continue

        def sent(turn, none):
            direct(hop, turn).wait_send()
            return none

        lax.fori_loop(1 if hop == 0 else 0, RING, sent, 0)

    def landed(n, none):
        sender = (place + n) % owners
        arrived(incoming.at[sender], sem_or.at[sender])
        return none

    lax.fori_loop(1, owners, landed, 0)
    for r in range(len(relays)):
        second_leg(r).wait_send()


def settle(source_ref, incoming_ref, attended_in, cache_ref, attended_ref, blank, sem, sem_two):
    rows = pltpu.make_async_copy(attended_in, attended_ref, sem_two)
    rows.start()
    blank[...] = jnp.zeros_like(blank)
    pages = cache_ref.shape[0]

    def begin(n, none):
        source = source_ref[0, n]

        @pl.when(source >= 0)
        def _():
            pltpu.make_async_copy(incoming_ref.at[source], cache_ref.at[n], sem).start()

        @pl.when(source < 0)
        def _():
            pltpu.make_async_copy(blank, cache_ref.at[n], sem).start()

        return none

    lax.fori_loop(0, pages, begin, 0, unroll=4)
    pltpu.make_async_copy(incoming_ref, cache_ref, sem).wait()
    rows.wait()


VMEM = pl.BlockSpec(memory_space=pltpu.VMEM)
SMEM = pl.BlockSpec(memory_space=pltpu.SMEM)
HBM = pl.BlockSpec(memory_space=pltpu.HBM)


def in_hbm(array):
    return pltpu.with_memory_space_constraint(array, pltpu.HBM)


def shards(query_rows, key_rows, value_rows, log_gate, norm_gain, doc_ends, doc_page):
    tokens, heads, depth = query_rows.shape
    width = value_rows.shape[2]
    devices, ranks = lax.axis_size("seq"), lax.axis_size("head")
    bounds = doc_ends.shape[0]
    groups = devices // RING
    quarter = depth // RING
    tiles = tokens // TILE
    table = doc_page.reshape(devices * bounds // TILE, TILE)
    dma = pltpu.SemaphoreType.DMA
    incoming, attended, source = pl.pallas_call(
        functools.partial(whole, groups, ranks, heads * ranks * width),
        out_shape=(
            jax.ShapeDtypeStruct((devices, depth, width), BF16),
            jax.ShapeDtypeStruct((tokens, width), BF16),
            jax.ShapeDtypeStruct((1, devices), jnp.int32),
        ),
        in_specs=[HBM] * 7,
        out_specs=(VMEM, VMEM, VMEM),
        scratch_shapes=[
            pltpu.VMEM((tokens, depth), BF16),
            pltpu.VMEM((tokens, depth), BF16),
            pltpu.VMEM((tokens, width), BF16),
            pltpu.VMEM((tiles, TILE), F32),
            pltpu.VMEM(table.shape, jnp.int32),
            pltpu.VMEM((1, bounds), jnp.int32),
            pltpu.VMEM((1, width), F32),
            pltpu.VMEM((devices, depth, width), BF16),
            pltpu.VMEM((RING, depth, width), BF16),
            pltpu.VMEM((tokens, width), F32),
            pltpu.VMEM((tiles, TILE), F32),
            pltpu.VMEM((tiles, TILE), F32),
            pltpu.VMEM((1, tokens), F32),
            pltpu.VMEM((tiles, TILE), F32),
            pltpu.VMEM((ranks, tiles, TILE), F32),
            pltpu.VMEM((depth, tokens), BF16),
            pltpu.VMEM((depth, tokens), BF16),
            pltpu.VMEM((8 * depth, tokens), BF16),
            pltpu.VMEM((depth, width), F32),
            pltpu.VMEM((1, 1, TILE), F32),
            pltpu.VMEM((RING, quarter, width), F32),
            pltpu.VMEM((RING, 1, TILE), F32),
            pltpu.VMEM((quarter, width), BF16),
            pltpu.VMEM((1, 1, TILE), F32),
            pltpu.VMEM((groups, quarter, width), BF16),
            pltpu.VMEM((groups, 1, TILE), F32),
            pltpu.VMEM((RING, quarter, width), F32),
            pltpu.VMEM((RING, quarter, width), F32),
            pltpu.VMEM((depth, width), F32),
            dma((7,)),
            dma((RING,)),
            dma((RING,)),
            dma((RING,)),
            dma((RING,)),
            dma((groups,)),
            dma((groups,)),
            dma((groups,)),
            dma((groups,)),
            dma((RING,)),
            dma((RING,)),
            dma((ranks,)),
            dma((ranks,)),
            dma((devices,)),
            dma((devices,)),
            dma((RING,)),
            dma((RING,)),
            dma((RING,)),
        ],
        compiler_params=pltpu.CompilerParams(
            collective_id=0, has_side_effects=True, vmem_limit_bytes=40 << 20
        ),
        name="whole",
    )(
        in_hbm(query_rows.reshape(tokens, depth)),
        in_hbm(key_rows.reshape(tokens, depth)),
        in_hbm(value_rows.reshape(tokens, width)),
        in_hbm(log_gate.reshape(tiles, TILE)),
        in_hbm(doc_ends.reshape(1, bounds)),
        in_hbm(table),
        in_hbm(norm_gain),
    )
    cache, attended = pl.pallas_call(
        settle,
        out_shape=(
            jax.ShapeDtypeStruct((devices, depth, width), BF16),
            jax.ShapeDtypeStruct((tokens, width), BF16),
        ),
        in_specs=[SMEM, VMEM, VMEM],
        out_specs=(HBM, HBM),
        scratch_shapes=[
            pltpu.VMEM((depth, width), BF16),
            pltpu.SemaphoreType.DMA,
            pltpu.SemaphoreType.DMA,
        ],
        compiler_params=pltpu.CompilerParams(vmem_limit_bytes=8 << 20),
        name="settle",
    )(source, incoming, attended)
    return attended.reshape(tokens, heads, width), cache.reshape(devices, heads, depth, width)


def solution(mesh):
    placed = (
        P("seq", "head", None),
        P("seq", "head", None),
        P("seq", "head", None),
        P("head", "seq"),
        P("head", None),
        P("seq"),
        P(),
    )
    return jax.shard_map(
        shards,
        mesh=mesh,
        in_specs=placed,
        out_specs=(P("seq", "head", None), P("seq", "head", None, None)),
        check_vma=False,
    )
```

time: 158 us -> 133 us (0.84)
  Pallas kernels: 40.3 us -> 133 us
  waiting for transfers between devices: 75.3 us -> 0 us
  blocking collectives: 21.5 us -> 0 us
  starting transfers between devices: 12.9 us -> 0 us
  local copies, waits for them, and re-layouts: 7.12 us -> 0 us
    pallas_call x3 -> x2, Pallas kernels: 40.3 us -> 133 us  [the longest x1 131 us: shards(): pl.pallas_call(functools.partial(whole, groups, ranks, heads * ranks * wi...]
    all_to_all x1 -> x0, waiting for transfers between devices: 75.3 us -> none  [shards(): lax.all_to_all(slots, 'seq', split_axis=0, concat_axis=0, tiled=True)]
    psum x1 -> x0, blocking collectives: 21.5 us -> none  [shards(): squares = lax.psum(squares, 'head')]
    all_to_all x1 -> x0, starting transfers between devices: 12.9 us -> none  [shards(): lax.all_to_all(slots, 'seq', split_axis=0, concat_axis=0, tiled=True)]
    unnamed x16 -> x0, local copies, waits for them, and re-layouts: 6.33 us -> none
  transfers between devices with their start and end apart: 1 -> 0, of which waited for: 1 -> 0; matrix products, arithmetic and copies ran while one was open for 0% -> 0% of each run, Pallas kernels for 1% -> 0%
where the time goes in v2:
time: 133 us
  Pallas kernels  133 us (100%)
    pallas_call x1, Pallas kernels, shards(): pl.pallas_call(functools.partial(whole, groups, ranks, heads * ranks * wi...  131 us

profile of v2, /device:TPU:56, one launch (start us, length us, event | category | flops | bytes accessed | tf_op | source)
XLA Modules:
  0.0 133.2 jit_solution(15666575039515442265)
XLA Ops:
  0.6 130.6 %whole.1 = (bf16[64,128,128]{2,1,0:T(8,128)(2,1)S(1)}, bf16[1024,128]{1,0:T(8,128)(2,1)S(1)}, s32[1,64]{1,0:T(1,128)S(1)}) custom-call(bf16[1024,128]{1,0:T(8,128)(2,1)} %bitcast.10, bf16[1024,128]{1,0:T(8,128)(2,1)} %bitcast.11, bf16[1024,128]{1,0:T(8,128)(2,1)} %bitcast.12, f32[8,128]{1,0:T(8,128)} %bitcast.14, s32[1,64]{1,0:T(1,128)} %bitcast.15, ...), custom_call_target="tpu_custom_call" | custom-call | tf_op jit(solution)/shard_map/whole/pallas_call | solution.py:568
  131.2 1.9 %settle.1 = (bf16[64,128,128]{2,1,0:T(8,128)(2,1)}, bf16[1024,128]{1,0:T(8,128)(2,1)}) custom-call(s32[1,64]{1,0:T(1,128)S(1)} %get-tuple-element.7.source_ref, bf16[64,128,128]{2,1,0:T(8,128)(2,1)S(1)} %get-tuple-element.8.incoming_ref, bf16[1024,128]{1,0:T(8,128)(2,1)S(1)} %get-tuple-element.9.attended_in), custom_call_target="tpu_custom_call" | custom-call | tf_op jit(solution)/shard_map/settle/pallas_call | solution.py:639

commit v3 on v2

--- a/solution.py
+++ b/solution.py
@@ -80,7 +80,8 @@
     seg_rows,
     own_rows,
     squares,
-    head_squares,
+    head_out,
+    head_in,
     raw_t,
     scaled_t,
     lhs,
@@ -95,6 +96,7 @@
     back_out,
     back_in,
     first_state,
+    ready,
     sem_in,
     sem_xs,
     sem_xr,
@@ -142,18 +144,21 @@
 
     barrier = pltpu.get_barrier_semaphore()
 
-    def greet_seq(n, none):
-        device = ((place + n) % owners, head)
-        pl.semaphore_signal(barrier, inc=1, device_id=device, device_id_type=MESH)
-        return none
-
-    def greet_head(n, none):
-        device = (place, (head + n) % heads)
-        pl.semaphore_signal(barrier, inc=1, device_id=device, device_id_type=MESH)
-        return none
-
-    lax.fori_loop(1, owners, greet_seq, 0)
-    lax.fori_loop(1, heads, greet_head, 0)
+    spans = [1 << n for n in range((heads - 1).bit_length())]
+
+    def partner(span):
+        return head + span * (1 - 2 * ((head // span) % 2))
+
+    def greet(semaphore, device):
+        pl.semaphore_signal(semaphore, inc=1, device_id=device, device_id_type=MESH)
+
+    reach_out = sorted(range(1, groups), key=lambda n: -min(n, groups - n))
+    for hop in reach_out:
+        greet(barrier, (((z + hop) % groups) * RING + x, head))
+    for hop in (2, 1, 3):
+        greet(barrier, (z * RING + (x + hop) % RING, head))
+    for span in spans:
+        greet(barrier, (place, partner(span)))
 
     loads[0].wait()
     loads[1].wait()
@@ -215,7 +220,7 @@
     through = jnp.where(any_ended > 0.0, 0.0, jnp.exp(total))
     link[0] = jnp.broadcast_to(through, (1, TILE))
 
-    pl.semaphore_wait(barrier, owners + heads - 2)
+    pl.semaphore_wait(barrier, groups + RING - 2 + len(spans))
 
     def x_copies(hop):
         to = (x + hop) % RING
@@ -238,6 +243,8 @@
     for hop in (2, 1, 3):
         for copy in x_copies(hop):
             copy.start()
+    for hop in reach_out:
+        greet(ready, (((z + hop) % groups) * RING + x, head))
     mine = pl.ds(pl.multiple_of(x * quarter, quarter), quarter)
     x_state[x] = state[mine, :]
     x_link[x] = link[0]
@@ -263,7 +270,7 @@
             ),
         )
 
-    for hop in sorted(range(1, groups), key=lambda n: -min(n, groups - n)):
+    for hop in reach_out:
 
         @pl.when(z + hop < groups)
         def _():
@@ -381,6 +388,7 @@
         lax.fori_loop(1 if hop == 0 else 0, RING, one, 0)
 
     finish(order[0])
+    pl.semaphore_wait(ready, groups - 1)
     for n, hop in enumerate(order):
         if n + 1 < len(order):
             finish(order[n + 1])
@@ -424,23 +432,6 @@
 
     lax.fori_loop(0, tiles, attend, 0)
 
-    def square_copy(n):
-        return pltpu.make_async_remote_copy(
-            squares,
-            head_squares.at[head],
-            sem_hs.at[n],
-            sem_hr.at[head],
-            (place, (head + n) % heads),
-            MESH,
-        )
-
-    def send_square(n, none):
-        square_copy(n).start()
-        return none
-
-    lax.fori_loop(1, heads, send_square, 0)
-    head_squares[head] = squares[...]
-
     for r in range(len(relays)):
         arrived(relay.at[r], sem_rr.at[r])
         second_leg(r).start()
@@ -465,15 +456,22 @@
         jnp.where(eye, jnp.broadcast_to(found, (owners, owners)), 0.0), axis=0, keepdims=True
     ).astype(jnp.int32)
 
-    def take_square(n, none):
-        sender = (head + n) % heads
-        arrived(head_squares.at[sender], sem_hr.at[sender])
-        return none
-
-    lax.fori_loop(1, heads, take_square, 0)
-    energy = head_squares[0]
-    for n in range(1, heads):
-        energy = energy + head_squares[n]
+    def square_copy(n):
+        return pltpu.make_async_remote_copy(
+            head_out.at[n],
+            head_in.at[n],
+            sem_hs.at[n],
+            sem_hr.at[n],
+            (place, partner(spans[n])),
+            MESH,
+        )
+
+    energy = squares[...]
+    for n in range(len(spans)):
+        head_out[n] = energy
+        square_copy(n).start()
+        square_copy(n).wait_recv()
+        energy = energy + head_in[n]
     cum_rows[...] = lax.rsqrt(energy / count + EPS)
 
     def normed(t, none):
@@ -495,11 +493,8 @@
             for copy in z_copies(hop):
                 copy.wait_send()
 
-    def sent_square(n, none):
+    for n in range(len(spans)):
         square_copy(n).wait_send()
-        return none
-
-    lax.fori_loop(1, heads, sent_square, 0)
     for hop in order:
         if hop == half and relays:
             for r in range(len(relays)):
@@ -589,7 +584,8 @@
             pltpu.VMEM((tiles, TILE), F32),
             pltpu.VMEM((1, tokens), F32),
             pltpu.VMEM((tiles, TILE), F32),
-            pltpu.VMEM((ranks, tiles, TILE), F32),
+            pltpu.VMEM((max(ranks.bit_length() - 1, 1), tiles, TILE), F32),
+            pltpu.VMEM((max(ranks.bit_length() - 1, 1), tiles, TILE), F32),
             pltpu.VMEM((depth, tokens), BF16),
             pltpu.VMEM((depth, tokens), BF16),
             pltpu.VMEM((8 * depth, tokens), BF16),
@@ -604,6 +600,7 @@
             pltpu.VMEM((RING, quarter, width), F32),
             pltpu.VMEM((RING, quarter, width), F32),
             pltpu.VMEM((depth, width), F32),
+            pltpu.SemaphoreType.REGULAR,
             dma((7,)),
             dma((RING,)),
             dma((RING,)),
@@ -615,8 +612,8 @@
             dma((groups,)),
             dma((RING,)),
             dma((RING,)),
-            dma((ranks,)),
-            dma((ranks,)),
+            dma((max(ranks.bit_length() - 1, 1),)),
+            dma((max(ranks.bit_length() - 1, 1),)),
             dma((devices,)),
             dma((devices,)),
             dma((RING,)),

time: 133 us -> 132 us (level)
  Pallas kernels: 133 us -> 131 us
    pallas_call x1, Pallas kernels: 131 us -> 129 us  [shards(): pl.pallas_call(functools.partial(whole, groups, ranks, heads * ranks * wi...]
where the time goes in v3:
time: 132 us; the launch traced here: 131 us
  Pallas kernels  131 us (99%)
    pallas_call x1, Pallas kernels, shards(): pl.pallas_call(functools.partial(whole, groups, ranks, heads * ranks * wi...  129 us

profile of v3, /device:TPU:56, one launch (start us, length us, event | category | flops | bytes accessed | tf_op | source)
XLA Modules:
  0.0 131.4 jit_solution(9356356850511189475)
XLA Ops:
  0.6 128.9 %whole.1 = (bf16[64,128,128]{2,1,0:T(8,128)(2,1)S(1)}, bf16[1024,128]{1,0:T(8,128)(2,1)S(1)}, s32[1,64]{1,0:T(1,128)S(1)}) custom-call(bf16[1024,128]{1,0:T(8,128)(2,1)} %bitcast.10, bf16[1024,128]{1,0:T(8,128)(2,1)} %bitcast.11, bf16[1024,128]{1,0:T(8,128)(2,1)} %bitcast.12, f32[8,128]{1,0:T(8,128)} %bitcast.14, s32[1,64]{1,0:T(1,128)} %bitcast.15, ...), custom_call_target="tpu_custom_call" | custom-call | tf_op jit(solution)/shard_map/whole/pallas_call | solution.py:563
  129.5 1.9 %settle.1 = (bf16[64,128,128]{2,1,0:T(8,128)(2,1)}, bf16[1024,128]{1,0:T(8,128)(2,1)}) custom-call(s32[1,64]{1,0:T(1,128)S(1)} %get-tuple-element.7.source_ref, bf16[64,128,128]{2,1,0:T(8,128)(2,1)S(1)} %get-tuple-element.8.incoming_ref, bf16[1024,128]{1,0:T(8,128)(2,1)S(1)} %get-tuple-element.9.attended_in), custom_call_target="tpu_custom_call" | custom-call | tf_op jit(solution)/shard_map/settle/pallas_call | solution.py:636

commit v4 on v3

--- a/solution.py
+++ b/solution.py
@@ -96,6 +96,7 @@
     back_out,
     back_in,
     first_state,
+    lead_out,
     ready,
     sem_in,
     sem_xs,
@@ -115,6 +116,9 @@
     sem_rs,
     sem_rr,
     sem_fs,
+    sem_cs,
+    sem_cr,
+    sem_cf,
 ):
     place = lax.axis_index("seq")
     head = lax.axis_index("head")
@@ -144,6 +148,9 @@
 
     barrier = pltpu.get_barrier_semaphore()
 
+    def target(hop, turn):
+        return ((z + hop + groups) % groups) * RING + (x + turn) % RING
+
     spans = [1 << n for n in range((heads - 1).bit_length())]
 
     def partner(span):
@@ -159,6 +166,11 @@
         greet(barrier, (z * RING + (x + hop) % RING, head))
     for span in spans:
         greet(barrier, (place, partner(span)))
+    ahead = max(1, 3 * groups // 16) if groups >= 4 else 0
+    ways = (ahead, -ahead) if ahead else ()
+    for way in ways:
+        for turn in range(1, RING):
+            greet(barrier, (target(way, turn), head))
 
     loads[0].wait()
     loads[1].wait()
@@ -220,7 +232,7 @@
     through = jnp.where(any_ended > 0.0, 0.0, jnp.exp(total))
     link[0] = jnp.broadcast_to(through, (1, TILE))
 
-    pl.semaphore_wait(barrier, groups + RING - 2 + len(spans))
+    pl.semaphore_wait(barrier, groups + RING - 2 + len(spans) + len(ways) * (RING - 1))
 
     def x_copies(hop):
         to = (x + hop) % RING
@@ -248,6 +260,27 @@
     mine = pl.ds(pl.multiple_of(x * quarter, quarter), quarter)
     x_state[x] = state[mine, :]
     x_link[x] = link[0]
+    def direct(hop, turn):
+        n = target(hop, turn)
+        return pltpu.make_async_remote_copy(
+            slots.at[n], incoming.at[place], sem_os.at[n], sem_or.at[place], (n, head), MESH
+        )
+
+    def build(planes):
+        for b, plane in enumerate(planes):
+            for turn in range(RING):
+                number = (plane * RING + turn).astype(F32)
+                mask = jnp.where(own_rows[...] == number, 1.0, 0.0).astype(BF16)
+                rows = pl.ds((b * RING + turn) * depth, depth)
+                lhs[rows, :] = scaled_t[...] * mask
+        count_rows = len(planes) * RING * depth
+        result = jnp.dot(lhs[0:count_rows, :], v_ref[...], preferred_element_type=F32)
+        result = result.astype(BF16).reshape(len(planes) * RING, depth, v_ref.shape[1])
+        for b, plane in enumerate(planes):
+            slots[pl.ds(plane * RING, RING)] = result[b * RING : (b + 1) * RING]
+
+    if ways:
+        build([(z + way + groups) % groups for way in ways])
     for hop in range(1, RING):
         sender = (x + hop) % RING
         arrived(x_state.at[sender], sem_xr.at[sender])
@@ -277,19 +310,24 @@
             for copy in z_copies(hop):
                 copy.start()
 
+    for turn in range(RING):
+        for way in ways:
+            direct(way, turn).start()
+
     own_all = own_rows[...]
-    batch = lhs.shape[0] // depth
-
-    def slot_group(n, carry):
-        for b in range(batch):
-            number = (n * batch + b).astype(F32)
-            mask = jnp.where(own_rows[...] == number, 1.0, 0.0).astype(BF16)
-            lhs[pl.ds(b * depth, depth), :] = scaled_t[...] * mask
-        result = jnp.dot(lhs[...], v_ref[...], preferred_element_type=F32)
-        slots[pl.ds(n * batch, batch)] = result.astype(BF16).reshape(batch, depth, v_ref.shape[1])
-        return carry
-
-    lax.fori_loop(0, owners // batch, slot_group, 0)
+
+    def remaining(n):
+        if not ways:
+            return n
+        n = n + jnp.where(n >= ahead, 1, 0)
+        n = n + jnp.where(n >= groups - ahead, 1, 0)
+        return (z + n) % groups
+
+    def slot_group(n, none):
+        build([remaining(2 * n), remaining(2 * n + 1)])
+        return none
+
+    lax.fori_loop(0, (groups - len(ways)) // 2, slot_group, 0)
     leading = jnp.where((jnp.concatenate(seg_row, axis=1) == 0.0) & (own_all >= 0.0), 1.0, 0.0)
     first_state[...] = jnp.dot(
         scaled_t[...] * leading.astype(BF16), v_ref[...], preferred_element_type=F32
@@ -326,14 +364,12 @@
     carry = back_in[...].reshape(depth, v_ref.shape[1])
     lead_owner = jnp.where(ends[0:1, :] > 0.0, owner[0:1, :], -1.0)
     lead = (first_state[...] + jnp.exp(at_end[0:1, :]) * carry).astype(BF16)
+    lead_out[...] = lead
 
     half, step_off = groups // 2, groups // 4
     relays = tuple((n, -1 if n % 2 == 0 else 1) for n in range(RING)) if step_off else ()
-    order = order_of(groups)
-    early = len(order) * 9 // 16
-
-    def target(hop, turn):
-        return ((z + hop + groups) % groups) * RING + (x + turn) % RING
+    order = [hop for hop in order_of(groups) if hop not in ways]
+    early = (len(order) + 1) // 2
 
     def finish(hop):
         def one(turn, none):
@@ -345,10 +381,26 @@
 
         lax.fori_loop(0, RING, one, 0)
 
-    def direct(hop, turn):
-        n = target(hop, turn)
+    def lead_copy(n):
+        spot = owners + n * RING + x
         return pltpu.make_async_remote_copy(
-            slots.at[n], incoming.at[place], sem_os.at[n], sem_or.at[place], (n, head), MESH
+            lead_out,
+            incoming.at[spot],
+            sem_cs.at[n],
+            sem_cr.at[n * RING + x],
+            (target(ways[n], 0), head),
+            MESH,
+        )
+
+    def lead_spread(n, turn):
+        spot = owners + n * RING + x
+        return pltpu.make_async_remote_copy(
+            incoming.at[spot],
+            incoming.at[spot],
+            sem_cf.at[n * RING + turn],
+            sem_cr.at[n * RING + x],
+            (target(0, turn), head),
+            MESH,
         )
 
     def first_leg(r):
@@ -389,6 +441,8 @@
 
     finish(order[0])
     pl.semaphore_wait(ready, groups - 1)
+    for n in range(len(ways)):
+        lead_copy(n).start()
     for n, hop in enumerate(order):
         if n + 1 < len(order):
             finish(order[n + 1])
@@ -435,20 +489,33 @@
     for r in range(len(relays)):
         arrived(relay.at[r], sem_rr.at[r])
         second_leg(r).start()
+    for n in range(len(ways)):
+        arrived(incoming.at[owners + n * RING + x], sem_cr.at[n * RING + x])
+        for turn in range(1, RING):
+            lead_spread(n, turn).start()
     for hop in order[early:]:
         fire(hop)
 
     fold_rows = table_ref.shape[0]
     page_lane = lax.broadcasted_iota(jnp.int32, (owners, TILE), 1)
     wanted = lax.broadcasted_iota(jnp.int32, (owners, TILE), 0) + place * owners
-    which = (page_lane // docs).astype(F32)
+    which = (page_lane // docs + jnp.where(page_lane % docs == 0, owners, 0)).astype(F32)
 
     def search(n, found):
         row = table_ref[pl.ds(n, 1), :]
         return jnp.where(row == wanted, which + (n * fold).astype(F32), found)
 
     found = lax.fori_loop(0, fold_rows, search, jnp.full((owners, TILE), -1.0, F32))
-    found = jnp.max(found, axis=1, keepdims=True)
+    found = jnp.max(found, axis=1, keepdims=True).astype(jnp.int32)
+    leads_here = found >= owners
+    sender_of = jnp.where(leads_here, found - owners, found)
+    plane_of = sender_of >> (RING.bit_length() - 1)
+    column_of = sender_of - plane_of * RING
+    found = sender_of
+    for n, way in enumerate(ways):
+        match = leads_here & (plane_of == (z - way + groups) % groups)
+        found = jnp.where(match, owners + n * RING + column_of, found)
+    found = found.astype(F32)
     eye = lax.broadcasted_iota(jnp.int32, (owners, owners), 0) == lax.broadcasted_iota(
         jnp.int32, (owners, owners), 1
     )
@@ -495,7 +562,7 @@
 
     for n in range(len(spans)):
         square_copy(n).wait_send()
-    for hop in order:
+    for hop in list(ways) + order:
         if hop == half and relays:
             for r in range(len(relays)):
                 first_leg(r).wait_send()
@@ -515,6 +582,12 @@
     lax.fori_loop(1, owners, landed, 0)
     for r in range(len(relays)):
         second_leg(r).wait_send()
+    for n in range(len(ways)):
+        lead_copy(n).wait_send()
+        for turn in range(1, RING):
+            lead_spread(n, turn).wait_send()
+            sender = (x + turn) % RING
+            arrived(incoming.at[owners + n * RING + sender], sem_cr.at[n * RING + sender])
 
 
 def settle(source_ref, incoming_ref, attended_in, cache_ref, attended_ref, blank, sem, sem_two):
@@ -537,7 +610,7 @@
         return none
 
     lax.fori_loop(0, pages, begin, 0, unroll=4)
-    pltpu.make_async_copy(incoming_ref, cache_ref, sem).wait()
+    pltpu.make_async_copy(incoming_ref.at[pl.ds(0, pages)], cache_ref, sem).wait()
     rows.wait()
 
 
@@ -563,7 +636,7 @@
     incoming, attended, source = pl.pallas_call(
         functools.partial(whole, groups, ranks, heads * ranks * width),
         out_shape=(
-            jax.ShapeDtypeStruct((devices, depth, width), BF16),
+            jax.ShapeDtypeStruct((devices + 2 * RING, depth, width), BF16),
             jax.ShapeDtypeStruct((tokens, width), BF16),
             jax.ShapeDtypeStruct((1, devices), jnp.int32),
         ),
@@ -600,6 +673,7 @@
             pltpu.VMEM((RING, quarter, width), F32),
             pltpu.VMEM((RING, quarter, width), F32),
             pltpu.VMEM((depth, width), F32),
+            pltpu.VMEM((depth, width), BF16),
             pltpu.SemaphoreType.REGULAR,
             dma((7,)),
             dma((RING,)),
@@ -619,6 +693,9 @@
             dma((RING,)),
             dma((RING,)),
             dma((RING,)),
+            dma((2,)),
+            dma((2 * RING,)),
+            dma((2 * RING,)),
         ],
         compiler_params=pltpu.CompilerParams(
             collective_id=0, has_side_effects=True, vmem_limit_bytes=40 << 20

time: 132 us -> 128 us (0.970)
  Pallas kernels: 131 us -> 127 us
    pallas_call x1, Pallas kernels: 129 us -> 125 us  [shards(): pl.pallas_call(functools.partial(whole, groups, ranks, heads * ranks * wi...]
where the time goes in v4:
time: 128 us
  Pallas kernels  127 us (99%)
    pallas_call x1, Pallas kernels, shards(): pl.pallas_call(functools.partial(whole, groups, ranks, heads * ranks * wi...  125 us

profile of v4, /device:TPU:56, one launch (start us, length us, event | category | flops | bytes accessed | tf_op | source)
XLA Modules:
  0.0 127.6 jit_solution(2173307360987756739)
XLA Ops:
  0.6 125.0 %whole.1 = (bf16[72,128,128]{2,1,0:T(8,128)(2,1)S(1)}, bf16[1024,128]{1,0:T(8,128)(2,1)S(1)}, s32[1,64]{1,0:T(1,128)S(1)}) custom-call(bf16[1024,128]{1,0:T(8,128)(2,1)} %bitcast.10, bf16[1024,128]{1,0:T(8,128)(2,1)} %bitcast.11, bf16[1024,128]{1,0:T(8,128)(2,1)} %bitcast.12, f32[8,128]{1,0:T(8,128)} %bitcast.14, s32[1,64]{1,0:T(1,128)} %bitcast.15, ...), custom_call_target="tpu_custom_call" | custom-call | tf_op jit(solution)/shard_map/whole/pallas_call | solution.py:636
  125.6 1.9 %settle.1 = (bf16[64,128,128]{2,1,0:T(8,128)(2,1)}, bf16[1024,128]{1,0:T(8,128)(2,1)}) custom-call(s32[1,64]{1,0:T(1,128)S(1)} %get-tuple-element.7.source_ref, bf16[72,128,128]{2,1,0:T(8,128)(2,1)S(1)} %get-tuple-element.8.incoming_ref, bf16[1024,128]{1,0:T(8,128)(2,1)S(1)} %get-tuple-element.9.attended_in), custom_call_target="tpu_custom_call" | custom-call | tf_op jit(solution)/shard_map/settle/pallas_call | solution.py:713
